TPU v7x, 256 devices: a whole 4x4x8 slice. The times are simulated.
256 devices in a mesh: col: 8 (over z), leaf: 32 (over y, x, core).
Axes of the slice: x: 4, y: 4, z: 8, core: 2. Of those that a mesh axis runs over, the one named last changes fastest.
Arguments:
- voltage: bfloat16 [128, 128, 4, 2048], P(None, 'leaf', None, 'col'), may hold values from -4 to 4
- source: bfloat16 [128, 128, 4, 2048], P(None, 'leaf', None, 'col'), may hold values from -6 to 6
- conduct: float32 [128, 4, 2048], P('leaf', None, 'col'), may hold values from 0.25 to 2
- leaf_inverse: bfloat16 [128, 4, 2048, 256], P('leaf', None, 'col'), as said below
- update_rows: int32 [8, 128, 4, 2], P('col', 'leaf'), may hold values from 0 to 127, as said below
- update_matrix: bfloat16 [128, 4, 256, 2048], P('leaf', None, None, 'col'), may hold values from -0.1875 to 0.1875
- chain_slot: int32 [64], replicated, may hold values from 0 to 63, as said below
- separator_source: float32 [128, 64, 2048], P(None, 'leaf', 'col'), may hold values from -6 to 6
- separator_inverse: float32 [64, 2048, 256], P('leaf', 'col'), as said below
- separator_coupling: float32 [64, 2048, 256], P('leaf', 'col'), may hold values from -0.3125 to 0.3125
Outputs:
- leaf_result: float32 [128, 128, 4, 2048], P(None, 'leaf', None, 'col')
- separator_result: float32 [128, 64, 2048], P(None, 'leaf', 'col')
Inputs may be any that keep to these rules, and one draw needn't show every extreme that they name: `update_rows`: row [q, x, y] names 2 different update-row blocks of the separator panels at position q; block t holds rows (t % 2) * 128 onward of chain t // 2. Among the 32 entries of the rows [q, x, y] held by one device, at most 2 name blocks whose chains are stored in storage rows i * 2 to (i + 1) * 2 - 1 for one i, and exactly 2 do for some i on every device. A permutation: chain j is stored at row chain_slot[j] of the separator arrays. `leaf_inverse`: each 256 x 256 block is a given inverse of a diagonal block. `separator_inverse`: each 256 x 256 block is a given inverse of a diagonal block.
All inputs are finite; a program needn't handle non-finite values.
Results may differ from a plain program's by a relative error of at most 0.0039.
Values may be sent and summed in bfloat16 or wider, within the bound.
No kernel may reach another device: no remote copies, remote signals or barrier semaphores. Data moves between devices by JAX's collectives and lax.ppermute only.
A program may use at most 128 MiB of HBM per device.

v0:
```python
import jax
import jax.numpy as jnp
from jax import lax
from jax.sharding import PartitionSpec as P


def padded_2(shard, sides, width):
    edges = {}
    for axis, dim in sides:
        size, length = (lax.axis_size(axis), shard.shape[dim])
        up = [(i, (i + 1) % size) for i in range(size - 1)]
        last = lax.slice_in_dim(shard, length - width, length, axis=dim)
        first = lax.slice_in_dim(shard, 0, width, axis=dim)
        edges[dim] = (
            lax.ppermute(last, axis, up),
            lax.ppermute(first, axis, [(b, a) for a, b in up]),
        )
    done = []
    for _, dim in sides:
        low, high = edges[dim]
        around = [(width, width) if d in done else (0, 0) for d in range(shard.ndim)]
        shard = jnp.concatenate([jnp.pad(low, around), shard, jnp.pad(high, around)], axis=dim)
        done.append(dim)
    return shard


def shifted(block, axis, distance):
    devices = range(lax.axis_size(axis))
    route = [(i - distance, i) for i in devices if i - distance in devices]
    return lax.ppermute(block, axis, route)


def body(
    voltage,
    source,
    conduct,
    leaf_inverse,
    update_rows,
    update_matrix,
    chain_slot,
    separator_source,
    separator_inverse,
    separator_coupling,
):
    highest = lax.Precision.HIGHEST
    fields, extent_x, extent_y, panel_width = voltage.shape
    per_leaf = update_rows.shape[3]
    block_rows = update_matrix.shape[2] // per_leaf
    halves = panel_width // block_rows
    panels = extent_x * extent_y
    chains = chain_slot.shape[0]
    sep_rows = separator_source.shape[1]
    padded = padded_2(voltage, (("col", 3), ("leaf", 1)), 1)
    widened = padded.astype(jnp.float32)
    center = widened[:, 1:-1, :, 1:-1]
    beside = widened[:, 2:, :, 1:-1] + widened[:, :-2, :, 1:-1]
    beside = beside + widened[:, 1:-1, :, 2:] + widened[:, 1:-1, :, :-2]
    y_padded = jnp.pad(center, ((0, 0), (0, 0), (1, 1), (0, 0)))
    beside = beside + y_padded[:, :, 2:, :] + y_padded[:, :, :-2, :]
    residual = source.astype(jnp.float32) - ((6.0 + conduct) * center - beside)
    residual_low = residual.astype(jnp.bfloat16).reshape(fields, panels, panel_width)
    inverse = leaf_inverse.reshape(panels, panel_width, panel_width)
    leaf_scaled = jnp.einsum(
        "pab,npb->npa", inverse, residual_low, preferred_element_type=jnp.float32
    )
    blocks = update_matrix.reshape(panels, per_leaf, block_rows, panel_width)
    contrib = jnp.einsum("pkjb,npb->pknj", blocks, residual_low, preferred_element_type=jnp.float32)
    targets = update_rows.reshape(panels, per_leaf)
    chain_hit = (targets // halves)[:, :, None] == jnp.arange(chains, dtype=jnp.int32)
    target_slot = jnp.sum(jnp.where(chain_hit, chain_slot, 0), axis=2)
    target_half = targets % halves
    half_hit = (target_half[:, :, None] == jnp.arange(halves, dtype=jnp.int32)).astype(jnp.float32)
    owners = lax.axis_size("leaf")
    entries = panels * per_leaf
    capacity = max(2, (entries + owners - 1) // owners)
    flat_slot = target_slot.reshape(entries)
    flat_owner = flat_slot // sep_rows
    flat_local = flat_slot % sep_rows * halves + target_half.reshape(entries)
    entry_ids = jnp.arange(entries, dtype=jnp.int32)
    same_owner = flat_owner[:, None] == flat_owner[None, :]
    earlier = entry_ids[None, :] < entry_ids[:, None]
    rank = jnp.sum((same_owner & earlier).astype(jnp.int32), axis=1)
    owner_hit = (flat_owner[None, :] == jnp.arange(owners, dtype=jnp.int32)[:, None]).astype(
        jnp.float32
    )
    rank_hit = (rank[None, :] == jnp.arange(capacity, dtype=jnp.int32)[:, None]).astype(jnp.float32)
    selector = owner_hit[:, None, :] * rank_hit[None, :, :]
    flat_contrib = contrib.reshape(entries, fields, block_rows)
    outgoing = jnp.einsum("dce,enj->dcnj", selector, flat_contrib, precision=highest)
    out_tags = (
        jnp.sum(selector * (flat_local.astype(jnp.float32) + 1.0)[None, None, :], axis=2) - 1.0
    )
    incoming, in_tags = (
        lax.all_to_all(outgoing, "leaf", split_axis=0, concat_axis=0, tiled=True),
        lax.all_to_all(out_tags, "leaf", split_axis=0, concat_axis=0, tiled=True),
    )
    local_hit = (in_tags[:, :, None] == jnp.arange(sep_rows * halves, dtype=jnp.float32)).astype(
        jnp.float32
    )
    gathered = jnp.einsum("scm,scnj->mnj", local_hit, incoming, precision=highest)
    gathered = gathered.reshape(sep_rows, halves, fields, block_rows)
    owned_sums = jnp.transpose(gathered, (0, 2, 1, 3)).reshape(sep_rows, fields, panel_width)
    chain_drive = jnp.transpose(separator_source, (1, 0, 2)) - owned_sums
    column_index = lax.axis_index("col")
    columns = lax.axis_size("col")
    coupling = jnp.where(column_index > 0, separator_coupling, 0.0)

    def push_down(values):
        return jnp.einsum("eab,enb->ena", coupling, values, precision=highest)

    def push_up(values):
        return jnp.einsum("eba,enb->ena", coupling, values, precision=highest)

    def step_down(sweep_turn, values):
        return chain_drive - push_down(shifted(values, "col", 1))

    forward_values = lax.fori_loop(0, columns - 1, step_down, chain_drive)
    chain_scaled = jnp.einsum("eab,enb->ena", separator_inverse, forward_values, precision=highest)

    def step_up(sweep_turn, values):
        return chain_scaled - shifted(push_up(values), "col", -1)

    backward_values = lax.fori_loop(0, columns - 1, step_up, chain_scaled)
    separator_result = jnp.transpose(backward_values, (1, 0, 2))
    separator_low = backward_values.astype(jnp.bfloat16)
    half_low = half_hit.astype(jnp.bfloat16)
    shard_piece = lax.all_gather(separator_low, "leaf", axis=0, tiled=True)
    row_count = shard_piece.shape[0]
    slot_hit = (target_slot[:, :, None] == jnp.arange(row_count, dtype=jnp.int32)).astype(
        jnp.bfloat16
    )
    selector = slot_hit[:, :, :, None] * half_low[:, :, None, :]
    split_rows = shard_piece.reshape(row_count, fields, halves, block_rows)
    picked = jnp.einsum("pksh,snhj->pknj", selector, split_rows, preferred_element_type=jnp.float32)
    correction = jnp.einsum(
        "pkjb,pknj->npb", blocks, picked.astype(jnp.bfloat16), preferred_element_type=jnp.float32
    )
    leaf_result = (leaf_scaled - correction).reshape(fields, extent_x, extent_y, panel_width)
    return (leaf_result, separator_result)


def solution(mesh):
    placed = (
        P(None, "leaf", None, "col"),
        P(None, "leaf", None, "col"),
        P("leaf", None, "col"),
        P("leaf", None, "col", None),
        P("col", "leaf", None, None),
        P("leaf", None, None, "col"),
        P(),
        P(None, "leaf", "col"),
        P("leaf", "col", None),
        P("leaf", "col", None),
    )
    return jax.shard_map(
        body,
        mesh=mesh,
        in_specs=placed,
        out_specs=(P(None, "leaf", None, "col"), P(None, "leaf", "col")),
        check_vma=False,
    )
```

profile of v0, /device:TPU:1, one launch (start us, length us, event | category | flops | bytes accessed | tf_op | source)
XLA Modules:
  0.0 361.1 jit_solution(15282674338685063201)
XLA Ops:
  9.9 5.2 %collective-permute-start.3 = (bf16[128,4,4,1]{3,2,1,0:T(4,128)(2,1)}, bf16[128,4,4,1]{3,2,1,0:T(4,128)(2,1)}, u32[]{:S(2)}, u32[]{:S(2)}) collective-permute-start(bf16[128,4,4,1]{3,2,1,0:T(4,128)(2,1)} %get-tuple-element.74), channel_id=1, source_target_pairs={{0,32},{32,64},{64,96},{96,128},{128,160},{160,192},{192,224},{1,3... | collective-permute-start | bytes 12296 | tf_op jit(solution)/shard_map/ppermute | solution.py:15
  25.0 7.7 %all-to-all-start = ((f32[32,1,2]{2,1,0:T(1,128)}), f32[32,1,2]{2,1,0:T(1,128)S(1)}, u32[]{:S(2)}, u32[]{:S(2)}) async-start(f32[32,1,2]{2,1,0:T(1,128)} %copy.71), calls=%async_computation | async-start | bytes 32768 | tf_op jit(solution)/shard_map/all_to_all | solution.py:95
  44.9 4.7 %fusion.14 = f32[32,2,128,128]{3,0,2,1:T(8,128)S(1)} fusion(f32[32,128,128]{2,1,0:T(8,128)S(1)} %bitcast.77, f32[2,32]{1,0:T(2,128)S(1)} %compare_convert_fusion.1, f32[32,32]{1,0:T(8,128)S(1)} %fusion.30), kind=kOutput, calls=%fused_computation.24 | convolution fusion | flops 402655232 | bytes 6295808 | tf_op jit(solution)/shard_map/dce,enj->dcnj/dot_general | solution.py:89
  49.5 5.2 %copy.75 = f32[32,2,128,128]{3,1,2,0:T(2,128)} copy(f32[32,2,128,128]{3,0,2,1:T(8,128)S(1)} %fusion.14) | data formatting | bytes 8388608 | tf_op jit(solution)/shard_map/dce,enj->dcnj/dot_general | solution.py:89
  54.7 7.6 %all-to-all-start.1 = ((f32[32,2,128,128]{3,1,2,0:T(2,128)}), f32[32,2,128,128]{3,1,2,0:T(2,128)}, u32[]{:S(2)}, u32[]{:S(2)}) async-start(f32[32,2,128,128]{3,1,2,0:T(2,128)} %copy.75), calls=%async_computation.1 | async-start | bytes 8388608 | tf_op jit(solution)/shard_map/all_to_all | solution.py:94
  62.7 50.3 %all-to-all-done.1 = f32[32,2,128,128]{3,1,2,0:T(2,128)} async-done(((f32[32,2,128,128]{3,1,2,0:T(2,128)}), f32[32,2,128,128]{3,1,2,0:T(2,128)}, u32[]{:S(2)}, u32[]{:S(2)}) %all-to-all-start.1) | async-done | bytes 4194336 | tf_op jit(solution)/shard_map/all_to_all | solution.py:94
  113.0 5.8 %fusion.4 = f32[4,128,128,1]{2,0,3,1:T(4,128)S(1)} fusion(f32[32,2,128,128]{3,1,2,0:T(2,128)} %all-to-all-done.1, f32[32,2]{0,1:T(2,128)S(1)} %bitcast.81), kind=kOutput, calls=%fused_computation.9 | convolution fusion | flops 50331904 | bytes 4456704 | tf_op jit(solution)/shard_map/scm,scnj->mnj/dot_general | solution.py:100
  119.2 65.2 %while.20 = (s32[]{:T(128)}, f32[2,128,256]{2,1,0:T(8,128)S(1)}, f32[2,256,256]{2,1,0:T(8,128)S(1)}, f32[2,128,256]{2,1,0:T(8,128)S(1)}, s32[]{:T(128)}) while((s32[]{:T(128)}, f32[2,128,256]{2,1,0:T(8,128)S(1)}, f32[2,256,256]{2,1,0:T(8,128)S(1)}, f32[2,128,256]{2,1,0:T(8,128)S(1)}, s32[]{:T(128)}) %tuple.43), condition=%wide.region_4.5_spmd, body=%wide.region_3.4_spmd.sunk | while | flops 201392128 | bytes 2359397 | solution.py:117
  143.2 4.4 %collective-permute-start = (f32[2,128,256]{2,1,0:T(8,128)S(1)}, f32[2,128,256]{2,1,0:T(8,128)S(1)}, u32[]{:S(2)}, u32[]{:S(2)}) collective-permute-start(f32[2,128,256]{2,1,0:T(8,128)S(1)} %get-tuple-element.136), channel_id=1, source_target_pairs={{0,32},{32,64},{64,96},{96,128},{128,160},{160,192},{192,224},{1,3... | collective-permute-start | bytes 786440 | tf_op jit(solution)/shard_map/while/body/eval_jaxpr/ppermute | solution.py:30
  156.6 4.8 %collective-permute-done = f32[2,128,256]{2,1,0:T(8,128)S(1)} collective-permute-done((f32[2,128,256]{2,1,0:T(8,128)S(1)}, f32[2,128,256]{2,1,0:T(8,128)S(1)}, u32[]{:S(2)}, u32[]{:S(2)}) %collective-permute-start) | collective-permute-done | bytes 262176 | tf_op jit(solution)/shard_map/while/body/eval_jaxpr/ppermute | solution.py:30
  166.4 5.5 %collective-permute-done = f32[2,128,256]{2,1,0:T(8,128)S(1)} collective-permute-done((f32[2,128,256]{2,1,0:T(8,128)S(1)}, f32[2,128,256]{2,1,0:T(8,128)S(1)}, u32[]{:S(2)}, u32[]{:S(2)}) %collective-permute-start) | collective-permute-done | bytes 262176 | tf_op jit(solution)/shard_map/while/body/eval_jaxpr/ppermute | solution.py:30
  172.5 5.2 %collective-permute-start = (f32[2,128,256]{2,1,0:T(8,128)S(1)}, f32[2,128,256]{2,1,0:T(8,128)S(1)}, u32[]{:S(2)}, u32[]{:S(2)}) collective-permute-start(f32[2,128,256]{2,1,0:T(8,128)S(1)} %get-tuple-element.136), channel_id=1, source_target_pairs={{0,32},{32,64},{64,96},{96,128},{128,160},{160,192},{192,224},{1,3... | collective-permute-start | bytes 786440 | tf_op jit(solution)/shard_map/while/body/eval_jaxpr/ppermute | solution.py:30
  177.7 6.1 %collective-permute-done = f32[2,128,256]{2,1,0:T(8,128)S(1)} collective-permute-done((f32[2,128,256]{2,1,0:T(8,128)S(1)}, f32[2,128,256]{2,1,0:T(8,128)S(1)}, u32[]{:S(2)}, u32[]{:S(2)}) %collective-permute-start) | collective-permute-done | bytes 262176 | tf_op jit(solution)/shard_map/while/body/eval_jaxpr/ppermute | solution.py:30
  186.2 72.0 %while.21 = (s32[]{:T(128)}, f32[2,128,256]{2,1,0:T(8,128)S(1)}, f32[2,256,256]{2,1,0:T(8,128)S(1)}, f32[2,128,256]{2,1,0:T(8,128)S(1)}, s32[]{:T(128)}) while((s32[]{:T(128)}, f32[2,128,256]{2,1,0:T(8,128)S(1)}, f32[2,256,256]{2,1,0:T(8,128)S(1)}, f32[2,128,256]{2,1,0:T(8,128)S(1)}, s32[]{:T(128)}) %tuple.51), condition=%wide.region_6.7_spmd, body=%wide.region_5.6_spmd.sunk | while | flops 201392128 | bytes 2883685 | solution.py:123
  188.6 8.1 %collective-permute-done.1 = f32[2,128,256]{2,1,0:T(8,128)S(1)} collective-permute-done((f32[2,128,256]{2,1,0:T(8,128)}, f32[2,128,256]{2,1,0:T(8,128)S(1)}, u32[]{:S(2)}, u32[]{:S(2)}) %collective-permute-start.1) | collective-permute-done | bytes 262176 | tf_op jit(solution)/shard_map/while/body/eval_jaxpr/ppermute | solution.py:30
  199.2 10.0 %collective-permute-done.1 = f32[2,128,256]{2,1,0:T(8,128)S(1)} collective-permute-done((f32[2,128,256]{2,1,0:T(8,128)}, f32[2,128,256]{2,1,0:T(8,128)S(1)}, u32[]{:S(2)}, u32[]{:S(2)}) %collective-permute-start.1) | collective-permute-done | bytes 262176 | tf_op jit(solution)/shard_map/while/body/eval_jaxpr/ppermute | solution.py:30
  211.7 8.6 %collective-permute-done.1 = f32[2,128,256]{2,1,0:T(8,128)S(1)} collective-permute-done((f32[2,128,256]{2,1,0:T(8,128)}, f32[2,128,256]{2,1,0:T(8,128)S(1)}, u32[]{:S(2)}, u32[]{:S(2)}) %collective-permute-start.1) | collective-permute-done | bytes 262176 | tf_op jit(solution)/shard_map/while/body/eval_jaxpr/ppermute | solution.py:30
  222.8 8.9 %collective-permute-done.1 = f32[2,128,256]{2,1,0:T(8,128)S(1)} collective-permute-done((f32[2,128,256]{2,1,0:T(8,128)}, f32[2,128,256]{2,1,0:T(8,128)S(1)}, u32[]{:S(2)}, u32[]{:S(2)}) %collective-permute-start.1) | collective-permute-done | bytes 262176 | tf_op jit(solution)/shard_map/while/body/eval_jaxpr/ppermute | solution.py:30
  234.2 6.0 %collective-permute-done.1 = f32[2,128,256]{2,1,0:T(8,128)S(1)} collective-permute-done((f32[2,128,256]{2,1,0:T(8,128)}, f32[2,128,256]{2,1,0:T(8,128)S(1)}, u32[]{:S(2)}, u32[]{:S(2)}) %collective-permute-start.1) | collective-permute-done | bytes 262176 | tf_op jit(solution)/shard_map/while/body/eval_jaxpr/ppermute | solution.py:30
  242.7 6.0 %collective-permute-done.1 = f32[2,128,256]{2,1,0:T(8,128)S(1)} collective-permute-done((f32[2,128,256]{2,1,0:T(8,128)}, f32[2,128,256]{2,1,0:T(8,128)S(1)}, u32[]{:S(2)}, u32[]{:S(2)}) %collective-permute-start.1) | collective-permute-done | bytes 262176 | tf_op jit(solution)/shard_map/while/body/eval_jaxpr/ppermute | solution.py:30
  251.2 7.0 %collective-permute-done.1 = f32[2,128,256]{2,1,0:T(8,128)S(1)} collective-permute-done((f32[2,128,256]{2,1,0:T(8,128)}, f32[2,128,256]{2,1,0:T(8,128)S(1)}, u32[]{:S(2)}, u32[]{:S(2)}) %collective-permute-start.1) | collective-permute-done | bytes 262176 | tf_op jit(solution)/shard_map/while/body/eval_jaxpr/ppermute | solution.py:30
  259.9 73.0 %all-gather.2.cloned.1.call-done = bf16[64,128,256]{2,1,0:T(8,128)(2,1)} async-done(((bf16[2,128,256]{2,1,0:T(8,128)(2,1)}), bf16[64,128,256]{2,1,0:T(8,128)(2,1)}) %all-gather.2.cloned.1.call-update) | async-done | bytes 4194320 | tf_op jit(solution)/shard_map/all_gather | solution.py:127
  332.9 6.4 %copy.78 = bf16[64,128,256]{1,2,0:T(8,128)(2,1)} copy(bf16[64,128,256]{2,1,0:T(8,128)(2,1)} %all-gather.2.cloned.1.call-done) | data formatting | bytes 8388608 | tf_op jit(solution)/shard_map/all_gather | solution.py:127
  339.3 6.6 %copy.79 = bf16[64,128,2,128]{3,0,2,1:T(8,128)(2,1)} copy(bf16[64,128,2,128]{1,3,2,0:T(8,128)(2,1)} %bitcast.74) | data formatting | bytes 8388608 | tf_op jit(solution)/shard_map/reshape | solution.py:133
  (108 shorter events, 93.4 us)
Async XLA Ops:
  7.2 36.7 %copy-start = (bf16[4,4,256,256]{3,2,1,0:T(8,128)(2,1)S(1)}, bf16[4,4,256,256]{3,2,1,0:T(8,128)(2,1)}, u32[]{:S(2)}) copy-start(bf16[4,4,256,256]{3,2,1,0:T(8,128)(2,1)} %param.19) | copy-start | bytes 6291460
  7.2 16.2 %copy-start.10 = (s32[64]{0:T(128)S(1)}, s32[64]{0:T(128)}, u32[]{:S(2)}) copy-start(s32[64]{0:T(128)} %param.20) | copy-start | bytes 772
  7.2 25.5 %copy-start.9 = (f32[4,4,256]{2,1,0:T(4,128)S(1)}, f32[4,4,256]{2,1,0:T(4,128)}, u32[]{:S(2)}) copy-start(f32[4,4,256]{2,1,0:T(4,128)} %param.16) | copy-start | bytes 49156
  9.9 22.8 %collective-permute-start.3 = (bf16[128,4,4,1]{3,2,1,0:T(4,128)(2,1)}, bf16[128,4,4,1]{3,2,1,0:T(4,128)(2,1)}, u32[]{:S(2)}, u32[]{:S(2)}) collective-permute-start(bf16[128,4,4,1]{3,2,1,0:T(4,128)(2,1)} %get-tuple-element.74), channel_id=1, source_target_pairs={{0,32},{32,64},{64,96},{96,128},{128,160},{160,192},{192,224},{1,3... | collective-permute-start | bytes 12296 | tf_op jit(solution)/shard_map/ppermute | solution.py:15
  15.1 17.6 %collective-permute-start.4 = (bf16[128,4,4,1]{3,2,1,0:T(4,128)(2,1)}, bf16[128,4,4,1]{3,2,1,0:T(4,128)(2,1)}, u32[]{:S(2)}, u32[]{:S(2)}) collective-permute-start(bf16[128,4,4,1]{3,2,1,0:T(4,128)(2,1)} %get-tuple-element.75), channel_id=1, source_target_pairs={{32,0},{64,32},{96,64},{128,96},{160,128},{192,160},{224,192},{33,... | collective-permute-start | bytes 12296 | tf_op jit(solution)/shard_map/ppermute | solution.py:16
  17.4 15.4 %collective-permute-start.2 = (bf16[128,1,4,256]{3,2,1,0:T(4,128)(2,1)}, bf16[128,1,4,256]{3,2,1,0:T(4,128)(2,1)S(1)}, u32[]{:S(2)}, u32[]{:S(2)}) collective-permute-start(bf16[128,1,4,256]{3,2,1,0:T(4,128)(2,1)} %get-tuple-element.76), channel_id=1, source_target_pairs={{0,1},{1,2},{2,3},{3,4},{4,5},{5,6},{6,7},{7,8},{8,9},{9,10},{10,1... | collective-permute-start | bytes 786440 | tf_op jit(solution)/shard_map/ppermute | solution.py:15
  21.3 11.4 %collective-permute-start.5 = (bf16[128,1,4,256]{3,2,1,0:T(4,128)(2,1)}, bf16[128,1,4,256]{3,2,1,0:T(4,128)(2,1)}, u32[]{:S(2)}, u32[]{:S(2)}) collective-permute-start(bf16[128,1,4,256]{3,2,1,0:T(4,128)(2,1)} %get-tuple-element.77), channel_id=1, source_target_pairs={{1,0},{2,1},{3,2},{4,3},{5,4},{6,5},{7,6},{8,7},{9,8},{10,9},{11,1... | collective-permute-start | bytes 786440 | tf_op jit(solution)/shard_map/ppermute | solution.py:16
  25.0 29.7 %all-to-all-start = ((f32[32,1,2]{2,1,0:T(1,128)}), f32[32,1,2]{2,1,0:T(1,128)S(1)}, u32[]{:S(2)}, u32[]{:S(2)}) async-start(f32[32,1,2]{2,1,0:T(1,128)} %copy.71), calls=%async_computation | async-start | bytes 32768 | tf_op jit(solution)/shard_map/all_to_all | solution.py:95
  54.7 58.3 %all-to-all-start.1 = ((f32[32,2,128,128]{3,1,2,0:T(2,128)}), f32[32,2,128,128]{3,1,2,0:T(2,128)}, u32[]{:S(2)}, u32[]{:S(2)}) async-start(f32[32,2,128,128]{3,1,2,0:T(2,128)} %copy.75), calls=%async_computation.1 | async-start | bytes 8388608 | tf_op jit(solution)/shard_map/all_to_all | solution.py:94
  62.3 270.6 %all-gather.2.cloned.1.call-start = ((), (), s32[]{:S(2)}) async-start(), calls=%async_computation.2 | async-start | bytes 4325376 | tf_op jit(solution)/shard_map/all_gather | solution.py:127
  119.2 7.6 %collective-permute-start = (f32[2,128,256]{2,1,0:T(8,128)S(1)}, f32[2,128,256]{2,1,0:T(8,128)S(1)}, u32[]{:S(2)}, u32[]{:S(2)}) collective-permute-start(f32[2,128,256]{2,1,0:T(8,128)S(1)} %get-tuple-element.136), channel_id=1, source_target_pairs={{0,32},{32,64},{64,96},{96,128},{128,160},{160,192},{192,224},{1,3... | collective-permute-start | bytes 786440 | tf_op jit(solution)/shard_map/while/body/eval_jaxpr/ppermute | solution.py:30
  127.4 7.1 %collective-permute-start = (f32[2,128,256]{2,1,0:T(8,128)S(1)}, f32[2,128,256]{2,1,0:T(8,128)S(1)}, u32[]{:S(2)}, u32[]{:S(2)}) collective-permute-start(f32[2,128,256]{2,1,0:T(8,128)S(1)} %get-tuple-element.136), channel_id=1, source_target_pairs={{0,32},{32,64},{64,96},{96,128},{128,160},{160,192},{192,224},{1,3... | collective-permute-start | bytes 786440 | tf_op jit(solution)/shard_map/while/body/eval_jaxpr/ppermute | solution.py:30
  135.2 7.4 %collective-permute-start = (f32[2,128,256]{2,1,0:T(8,128)S(1)}, f32[2,128,256]{2,1,0:T(8,128)S(1)}, u32[]{:S(2)}, u32[]{:S(2)}) collective-permute-start(f32[2,128,256]{2,1,0:T(8,128)S(1)} %get-tuple-element.136), channel_id=1, source_target_pairs={{0,32},{32,64},{64,96},{96,128},{128,160},{160,192},{192,224},{1,3... | collective-permute-start | bytes 786440 | tf_op jit(solution)/shard_map/while/body/eval_jaxpr/ppermute | solution.py:30
  143.2 8.5 %collective-permute-start = (f32[2,128,256]{2,1,0:T(8,128)S(1)}, f32[2,128,256]{2,1,0:T(8,128)S(1)}, u32[]{:S(2)}, u32[]{:S(2)}) collective-permute-start(f32[2,128,256]{2,1,0:T(8,128)S(1)} %get-tuple-element.136), channel_id=1, source_target_pairs={{0,32},{32,64},{64,96},{96,128},{128,160},{160,192},{192,224},{1,3... | collective-permute-start | bytes 786440 | tf_op jit(solution)/shard_map/while/body/eval_jaxpr/ppermute | solution.py:30
  152.4 9.0 %collective-permute-start = (f32[2,128,256]{2,1,0:T(8,128)S(1)}, f32[2,128,256]{2,1,0:T(8,128)S(1)}, u32[]{:S(2)}, u32[]{:S(2)}) collective-permute-start(f32[2,128,256]{2,1,0:T(8,128)S(1)} %get-tuple-element.136), channel_id=1, source_target_pairs={{0,32},{32,64},{64,96},{96,128},{128,160},{160,192},{192,224},{1,3... | collective-permute-start | bytes 786440 | tf_op jit(solution)/shard_map/while/body/eval_jaxpr/ppermute | solution.py:30
  162.1 9.8 %collective-permute-start = (f32[2,128,256]{2,1,0:T(8,128)S(1)}, f32[2,128,256]{2,1,0:T(8,128)S(1)}, u32[]{:S(2)}, u32[]{:S(2)}) collective-permute-start(f32[2,128,256]{2,1,0:T(8,128)S(1)} %get-tuple-element.136), channel_id=1, source_target_pairs={{0,32},{32,64},{64,96},{96,128},{128,160},{160,192},{192,224},{1,3... | collective-permute-start | bytes 786440 | tf_op jit(solution)/shard_map/while/body/eval_jaxpr/ppermute | solution.py:30
  172.5 11.3 %collective-permute-start = (f32[2,128,256]{2,1,0:T(8,128)S(1)}, f32[2,128,256]{2,1,0:T(8,128)S(1)}, u32[]{:S(2)}, u32[]{:S(2)}) collective-permute-start(f32[2,128,256]{2,1,0:T(8,128)S(1)} %get-tuple-element.136), channel_id=1, source_target_pairs={{0,32},{32,64},{64,96},{96,128},{128,160},{160,192},{192,224},{1,3... | collective-permute-start | bytes 786440 | tf_op jit(solution)/shard_map/while/body/eval_jaxpr/ppermute | solution.py:30
  187.3 9.3 %collective-permute-start.1 = (f32[2,128,256]{2,1,0:T(8,128)}, f32[2,128,256]{2,1,0:T(8,128)S(1)}, u32[]{:S(2)}, u32[]{:S(2)}) collective-permute-start(f32[2,128,256]{2,1,0:T(8,128)} %fusion.63), channel_id=1, source_target_pairs={{32,0},{64,32},{96,64},{128,96},{160,128},{192,160},{224,192},{33,... | collective-permute-start | bytes 786440 | tf_op jit(solution)/shard_map/while/body/eval_jaxpr/ppermute | solution.py:30
  197.9 11.3 %collective-permute-start.1 = (f32[2,128,256]{2,1,0:T(8,128)}, f32[2,128,256]{2,1,0:T(8,128)S(1)}, u32[]{:S(2)}, u32[]{:S(2)}) collective-permute-start(f32[2,128,256]{2,1,0:T(8,128)} %fusion.63), channel_id=1, source_target_pairs={{32,0},{64,32},{96,64},{128,96},{160,128},{192,160},{224,192},{33,... | collective-permute-start | bytes 786440 | tf_op jit(solution)/shard_map/while/body/eval_jaxpr/ppermute | solution.py:30
  210.4 9.9 %collective-permute-start.1 = (f32[2,128,256]{2,1,0:T(8,128)}, f32[2,128,256]{2,1,0:T(8,128)S(1)}, u32[]{:S(2)}, u32[]{:S(2)}) collective-permute-start(f32[2,128,256]{2,1,0:T(8,128)} %fusion.63), channel_id=1, source_target_pairs={{32,0},{64,32},{96,64},{128,96},{160,128},{192,160},{224,192},{33,... | collective-permute-start | bytes 786440 | tf_op jit(solution)/shard_map/while/body/eval_jaxpr/ppermute | solution.py:30
  221.5 10.2 %collective-permute-start.1 = (f32[2,128,256]{2,1,0:T(8,128)}, f32[2,128,256]{2,1,0:T(8,128)S(1)}, u32[]{:S(2)}, u32[]{:S(2)}) collective-permute-start(f32[2,128,256]{2,1,0:T(8,128)} %fusion.63), channel_id=1, source_target_pairs={{32,0},{64,32},{96,64},{128,96},{160,128},{192,160},{224,192},{33,... | collective-permute-start | bytes 786440 | tf_op jit(solution)/shard_map/while/body/eval_jaxpr/ppermute | solution.py:30
  232.9 7.3 %collective-permute-start.1 = (f32[2,128,256]{2,1,0:T(8,128)}, f32[2,128,256]{2,1,0:T(8,128)S(1)}, u32[]{:S(2)}, u32[]{:S(2)}) collective-permute-start(f32[2,128,256]{2,1,0:T(8,128)} %fusion.63), channel_id=1, source_target_pairs={{32,0},{64,32},{96,64},{128,96},{160,128},{192,160},{224,192},{33,... | collective-permute-start | bytes 786440 | tf_op jit(solution)/shard_map/while/body/eval_jaxpr/ppermute | solution.py:30
  241.4 7.3 %collective-permute-start.1 = (f32[2,128,256]{2,1,0:T(8,128)}, f32[2,128,256]{2,1,0:T(8,128)S(1)}, u32[]{:S(2)}, u32[]{:S(2)}) collective-permute-start(f32[2,128,256]{2,1,0:T(8,128)} %fusion.63), channel_id=1, source_target_pairs={{32,0},{64,32},{96,64},{128,96},{160,128},{192,160},{224,192},{33,... | collective-permute-start | bytes 786440 | tf_op jit(solution)/shard_map/while/body/eval_jaxpr/ppermute | solution.py:30
  249.9 8.2 %collective-permute-start.1 = (f32[2,128,256]{2,1,0:T(8,128)}, f32[2,128,256]{2,1,0:T(8,128)S(1)}, u32[]{:S(2)}, u32[]{:S(2)}) collective-permute-start(f32[2,128,256]{2,1,0:T(8,128)} %fusion.63), channel_id=1, source_target_pairs={{32,0},{64,32},{96,64},{128,96},{160,128},{192,160},{224,192},{33,... | collective-permute-start | bytes 786440 | tf_op jit(solution)/shard_map/while/body/eval_jaxpr/ppermute | solution.py:30
  (8 other events, 44.6 us)
Sparse Core Ops, SparseCore 0:
  259.0 73.8 all-gather.1
where the time goes:
time: 362 us; the launch traced here: 361 us
  waiting for transfers between devices  208 us (57%)
  starting transfers between devices  66.8 us (18%)
  local copies, waits for them, and re-layouts  31.4 us (9%)
  matrix products  29.8 us (8%)
  between operations  14.4 us (4%)
  other arithmetic  9.91 us (3%)
    ppermute x14, waiting for transfers between devices, shifted(): return lax.ppermute(block, axis, route)  85.1 us
    all_gather x1, waiting for transfers between devices, body(): shard_piece = lax.all_gather(separator_low, 'leaf', axis=0, tiled=True)  73 us
    all_to_all x1, waiting for transfers between devices, body(): lax.all_to_all(outgoing, 'leaf', split_axis=0, concat_axis=0, tiled=True)  50.3 us
    ppermute x14, starting transfers between devices, shifted(): return lax.ppermute(block, axis, route)  39 us
    ppermute x2, starting transfers between devices, padded_2(): lax.ppermute(last, axis, up)  9.1 us
    dot_general x7, matrix products, push_up(): return jnp.einsum('eba,enb->ena', coupling, values, precision=highest)  8.05 us
    all_to_all x1, starting transfers between devices, body(): lax.all_to_all(out_tags, 'leaf', split_axis=0, concat_axis=0, tiled=True)  7.72 us
    all_to_all x1, starting transfers between devices, body(): lax.all_to_all(outgoing, 'leaf', split_axis=0, concat_axis=0, tiled=True)  7.57 us
  transfers between devices with their start and end apart: 21, of which 16 were waited for; matrix products, arithmetic and copies ran while one was open for 7% of the time, Pallas kernels for 0%

commit v1 on v0

v1 whole, which is shorter than its diff:
```python
import functools
import jax
import jax.numpy as jnp
from jax import lax
from jax.experimental import pallas as pl
from jax.experimental.pallas import tpu as pltpu
from jax.sharding import PartitionSpec as P

VM = pl.BlockSpec(memory_space=pltpu.VMEM)
HB = pl.BlockSpec(memory_space=pltpu.HBM)
SM = pl.BlockSpec(memory_space=pltpu.SMEM)
F32 = jnp.float32
BF16 = jnp.bfloat16
MIB = 1 << 20
FACTOR_MIB = 56


def dot(a, b, kind):
    dims = {"nt": (((1,), (1,)), ((), ())), "nn": (((1,), (0,)), ((), ()))}[kind]
    return lax.dot_general(a, b, dims, preferred_element_type=F32)


def split(x):
    high = x.astype(BF16)
    return high, (x - high.astype(F32)).astype(BF16)


def dot3(a, b, kind):
    high, low = split(a)
    b_high, b_low = split(b)
    axis = 1 if kind == "nt" else 0
    left = jnp.concatenate([high, low, high], axis=1)
    right = jnp.concatenate([b_high, b_high, b_low], axis=axis)
    return dot(left, right, kind)


def leaf_kernel(extent_y, slot, volt, source, diag, below, above, left, right, blocks, marks, low_out, sent):
    panels, fields, width = volt.shape
    rows = sent.shape[2]
    per_leaf = slot.shape[0] // panels
    capacity = sent.shape[1] // fields
    sent[:, : capacity * fields, :] = jnp.zeros((sent.shape[0], capacity * fields, rows), BF16)
    sent[:, capacity * fields :, :] = marks[...]
    lane = lax.broadcasted_iota(jnp.int32, (fields, width), 1)
    rest = jnp.zeros((fields - 2 * panels, left.shape[1]), F32)
    sides = jnp.transpose(jnp.concatenate([left[...], right[...], rest], axis=0))
    for p in range(panels):
        y = p % extent_y
        center = volt[p].astype(F32)
        x_low = below[y] if p < extent_y else volt[p - extent_y]
        x_high = above[y] if p >= panels - extent_y else volt[p + extent_y]
        beside = x_high.astype(F32) + x_low.astype(F32)
        z_low = jnp.where(lane == 0, sides[:, p : p + 1], pltpu.roll(center, 1, 1))
        z_high = jnp.where(lane == width - 1, sides[:, panels + p : panels + p + 1], pltpu.roll(center, width - 1, 1))
        beside = beside + z_high + z_low
        if y + 1 < extent_y:
            beside = beside + volt[p + 1].astype(F32)
        if y > 0:
            beside = beside + volt[p - 1].astype(F32)
        residual = source[p].astype(F32) - (diag[p : p + 1, :] * center - beside)
        low = residual.astype(BF16)
        low_out[p] = low
        product = dot(low, blocks[p], "nt").astype(BF16)
        for k in range(per_leaf):
            s = slot[p * per_leaf + k]
            start = pl.multiple_of(lax.rem(s, capacity) * fields, fields)
            sent[lax.div(s, capacity), pl.ds(start, fields), :] = product[:, k * rows : (k + 1) * rows]


def scaled_kernel(low, inverse, out):
    for p in range(low.shape[0]):
        out[p] = dot(low[p], inverse[p], "nt")


def owner_kernel(capacity, received, own, drive, tags):
    sep_rows, fields, width = own.shape
    owners, _, rows = received.shape
    halves = width // rows
    count = sep_rows * halves
    step = 32

    def mark(s, r):
        return received[s, capacity * fields : capacity * fields + 16, :].astype(F32)[8 * r : 8 * r + 8]

    lane = lax.broadcasted_iota(jnp.int32, (1, rows), 1)
    for s in range(owners):
        line = mark(s, 0)[:1]
        for r in range(1, capacity):
            line = jnp.where(lane == r, mark(s, r)[:1], line)
        tags[s : s + 1, :] = line
    for c in range(fields // step):
        span = slice(c * step, (c + 1) * step)
        first = []
        for b in range(count):
            first.append(own[b // halves, span, (b % halves) * rows : (b % halves + 1) * rows])

        def add(s, totals):
            totals = list(totals)
            for r in range(capacity):
                tag = jnp.concatenate([mark(s, r)] * (step // 8), axis=0)
                start = r * fields + c * step
                block = received[s, start : start + step, :].astype(F32)
                for b in range(count):
                    totals[b] = totals[b] - jnp.where(tag == float(b), block, 0.0)
            return tuple(totals)

        totals = lax.fori_loop(0, owners, add, tuple(first), unroll=4)
        for b in range(count):
            drive[b // halves, span, (b % halves) * rows : (b % halves + 1) * rows] = totals[b].astype(BF16)


def pack_kernel(coupling, inverse, last_z, first_z, out):
    width = coupling.shape[2]
    for e in range(coupling.shape[0]):
        block = inverse[e]
        biggest = jnp.max(jnp.max(jnp.abs(block), axis=1, keepdims=True), axis=0, keepdims=True)
        power = jnp.clip(jnp.ceil(jnp.log2(biggest)), -120.0, 120.0)
        out[e, :width, :] = coupling[e]
        out[e, width : 2 * width, :] = block * jnp.exp2(-power)
        out[e, 2 * width : 2 * width + 8, :] = jnp.broadcast_to(power, (8, width))
        out[e, 2 * width + 8 :, :] = jnp.concatenate([last_z[...], first_z[...]], axis=1).astype(F32)


def factor_kernel(columns, place, *refs):
    pieces, (m_high, m_low, ring, z, y, sems) = refs[:columns], refs[columns:]
    chains, _, width = pieces[0].shape
    copies = [pltpu.make_async_copy(pieces[k], ring.at[k], sems.at[k]) for k in range(columns)]
    for copy in copies:
        copy.start()
    q = place[0]

    def at(p):
        return lax.rem(p - q + columns, columns)

    def coupling(rel, e):
        return ring[rel, e, :width, :]

    def inverse(rel, e):
        return ring[rel, e, width : 2 * width, :] * jnp.exp2(ring[rel, e, 2 * width : 2 * width + 1, :])

    row = lax.broadcasted_iota(jnp.int32, (width, width), 0)
    col = lax.broadcasted_iota(jnp.int32, (width, width), 1)
    eye = (row == col).astype(F32)
    copies[0].wait()
    for e in range(chains):
        z[q, e] = inverse(0, e)
        y[e] = eye
    for k in range(1, columns):
        copies[k].wait()

        @pl.when(q + k < columns)
        def _(k=k):
            out = [-dot3(y[e], coupling(k, e), "nt") for e in range(chains)]
            for e in range(chains):
                y[e] = out[e]
                z[q + k, e] = dot3(out[e], inverse(k, e), "nn")

    def put(p, xs):
        rel = at(p)
        for e in range(chains):
            high, low = split(xs[e])
            m_high[rel, e] = high
            m_low[rel, e] = low

    last = tuple(z[columns - 1, e] for e in range(chains))
    put(columns - 1, last)

    def up(i, xs):
        p = columns - 2 - i
        rel = at(p + 1)
        out = []
        for e in range(chains):
            x = -dot3(xs[e], coupling(rel, e), "nn")
            out.append(x + jnp.where(p >= q, z[p, e], 0.0))
        put(p, out)
        return tuple(out)

    lax.fori_loop(0, columns - 1, up, last)


def solve_kernel(columns, tag, m_high, m_low, *refs):
    drives, (result, sent, low) = refs[:columns], refs[columns:]
    sep_rows, fields, width = result.shape
    rows = sent.shape[2]
    halves = width // rows
    for e in range(sep_rows):
        acc = jnp.zeros((fields, width), F32)
        for k in range(columns):
            d = drives[k][e]
            acc = acc + dot(d, m_high[k, e], "nt") + dot(d, m_low[k, e], "nt")
        result[e] = acc
        narrow = acc.astype(BF16)
        for h in range(halves):
            low[e * halves + h] = narrow[:, h * rows : (h + 1) * rows]

    def pick(s, carry):
        sent[s] = low[jnp.maximum(tag[s], 0)]
        return carry

    lax.fori_loop(0, sent.shape[0], pick, 0, unroll=4)


def finish_kernel(extent_y, slot, scaled, blocks, received, out):
    panels, fields, width = scaled.shape
    lanes = width // 128
    group = out.shape[0] // fields
    per_leaf = slot.shape[0] // panels
    for p in range(panels):
        picked = [received[slot[p * per_leaf + k]] for k in range(per_leaf)]
        acc = scaled[p] - dot(jnp.concatenate(picked, axis=1), blocks[p], "nn")
        x, y = divmod(p, extent_y)
        for part in range(lanes):
            start = (x * lanes + part) * extent_y + y
            out[pl.ds(start, fields, stride=group), :] = acc[:, part * 128 : (part + 1) * 128]


def call(kernel, out_shape, in_specs, out_specs, limit, scratch=(), flops=0, moved=0):
    return pl.pallas_call(
        kernel,
        out_shape=out_shape,
        in_specs=in_specs,
        out_specs=out_specs,
        scratch_shapes=list(scratch),
        compiler_params=pltpu.CompilerParams(vmem_limit_bytes=limit * MIB),
        cost_estimate=pl.CostEstimate(flops=flops, bytes_accessed=moved, transcendentals=0),
    )


def level(
    voltage,
    source,
    conduct,
    leaf_inverse,
    update_rows,
    update_matrix,
    chain_slot,
    separator_source,
    separator_inverse,
    separator_coupling,
):
    fields, extent_x, extent_y, width = voltage.shape
    per_leaf = update_rows.shape[3]
    rows = update_matrix.shape[2] // per_leaf
    halves = width // rows
    panels = extent_x * extent_y
    chains = chain_slot.shape[0]
    sep_rows = separator_source.shape[1]
    owners = lax.axis_size("leaf")
    columns = lax.axis_size("col")
    entries = panels * per_leaf
    capacity = 2
    slots = owners * capacity
    shape = jax.ShapeDtypeStruct

    def shifted(block, axis, distance, wrap=False):
        size = lax.axis_size(axis)
        route = [(i, (i + distance) % size) for i in range(size) if wrap or 0 <= i + distance < size]
        return lax.ppermute(block, axis, route)

    fresh = lax.optimization_barrier(voltage)
    padded = call(
        pack_kernel,
        shape((sep_rows, 2 * width + 8 + panels, width), F32),
        [VM] * 4,
        VM,
        8,
        moved=2 << 20,
    )(
        separator_coupling,
        separator_inverse,
        jnp.transpose(fresh[:, :, :, width - 1].reshape(fields, panels)),
        jnp.transpose(fresh[:, :, :, 0].reshape(fields, panels)),
    )
    edges = (
        jnp.transpose(fresh[:, extent_x - 1], (1, 0, 2)),
        jnp.transpose(fresh[:, 0], (1, 0, 2)),
        padded.astype(jnp.float16),
    )
    last_x, first_x, packed = lax.optimization_barrier(edges)
    below = shifted(last_x, "leaf", 1)
    above = shifted(first_x, "leaf", -1)

    targets = update_rows.reshape(entries)
    chain_hit = (targets // halves)[:, None] == jnp.arange(chains, dtype=jnp.int32)
    target_slot = jnp.sum(jnp.where(chain_hit, chain_slot, 0), axis=1)
    owner = target_slot // sep_rows
    local = target_slot % sep_rows * halves + targets % halves
    ids = jnp.arange(entries, dtype=jnp.int32)
    same = (owner[:, None] == owner[None, :]) & (ids[None, :] < ids[:, None])
    slot = owner * capacity + jnp.sum(same.astype(jnp.int32), axis=1)
    slot_hit = slot[:, None] == jnp.arange(slots, dtype=jnp.int32)[None, :]
    out_tags = jnp.sum(jnp.where(slot_hit, local[:, None] + 1, 0), axis=0) - 1
    marks = jnp.broadcast_to(out_tags.astype(BF16).reshape(owners, capacity, 1, 1), (owners, capacity, 8, rows))
    marks = marks.reshape(owners, capacity * 8, rows)

    pieces = [padded] + [None] * (columns - 1)
    up = down = packed
    for hop in range(1, columns // 2):
        up = shifted(up, "col", 1, True)
        down = shifted(down, "col", -1, True)
        pieces[columns - hop] = up
        pieces[hop] = down
    column = lax.axis_index("col")
    left = pieces[columns - 1][0, 2 * width + 8 :, :fields].astype(F32)
    left = jnp.where(column > 0, left, 0.0)
    right = pieces[1][0, 2 * width + 8 :, fields : 2 * fields].astype(F32)
    right = jnp.where(column < columns - 1, right, 0.0)
    middle = sep_rows // 2
    up = shifted(up[:middle], "col", 1, True)
    down = shifted(down[middle:], "col", -1, True)
    for k in range(1, columns):
        if k != columns // 2:
            pieces[k] = pieces[k].astype(F32)
    pieces[columns // 2] = jnp.concatenate([up.astype(F32), down.astype(F32)], axis=0)

    blocks = update_matrix.reshape(panels, per_leaf * rows, width)
    inverse = leaf_inverse.reshape(panels, width, width)
    p_major = (1, 0, 2)
    low, sent = call(
        functools.partial(leaf_kernel, extent_y),
        (shape((panels, fields, width), BF16), shape((owners, capacity * fields + 16, rows), BF16)),
        [SM] + [VM] * 9,
        (VM, VM),
        12,
        flops=2 * panels * fields * width * width,
        moved=8 << 20,
    )(
        slot,
        jnp.transpose(voltage.reshape(fields, panels, width), p_major),
        jnp.transpose(source.reshape(fields, panels, width), p_major),
        (6.0 + conduct).reshape(panels, width),
        below,
        above,
        left,
        right,
        blocks,
        marks,
    )

    scaled = call(
        scaled_kernel,
        shape((panels, fields, width), F32),
        [VM, VM],
        VM,
        8,
        flops=2 * panels * fields * width * width,
        moved=6 << 20,
    )(low, inverse)

    def exchange(block):
        return lax.all_to_all(block, "leaf", split_axis=0, concat_axis=0, tiled=True)

    arrived = exchange(sent)
    drive, tags = call(
        functools.partial(owner_kernel, capacity),
        (shape((sep_rows, fields, width), BF16), shape((owners, rows), F32)),
        [VM, VM],
        (VM, VM),
        6,
        flops=slots * fields * rows,
        moved=3 << 20,
    )(arrived, jnp.transpose(separator_source, p_major))
    in_tags = tags[:, :capacity].reshape(slots).astype(jnp.int32)

    place = column.astype(jnp.int32).reshape(1)
    square = shape((columns, sep_rows, width, width), BF16)
    m_high, m_low = call(
        functools.partial(factor_kernel, columns),
        (square, square),
        [SM] + [HB] * columns,
        (VM, VM),
        FACTOR_MIB,
        scratch=[
            pltpu.VMEM((columns,) + packed.shape, F32),
            pltpu.VMEM((columns, sep_rows, width, width), F32),
            pltpu.VMEM((sep_rows, width, width), F32),
            pltpu.SemaphoreType.DMA((columns,)),
        ],
        flops=2 * 126 * width**3,
        moved=12 << 20,
    )(place, *pieces)

    drives = [drive] + [shifted(drive, "col", -k, True) for k in range(1, columns)]
    result, answer = call(
        functools.partial(solve_kernel, columns),
        (shape((sep_rows, fields, width), F32), shape((slots, fields, rows), BF16)),
        [SM] + [VM] * (2 + columns),
        (VM, VM),
        10,
        scratch=[pltpu.VMEM((sep_rows * halves, fields, rows), BF16)],
        flops=4 * columns * sep_rows * fields * width * width,
        moved=8 << 20,
    )(in_tags, m_high, m_low, *drives)
    returned = exchange(answer.reshape(owners, capacity, fields, rows)).reshape(slots, fields, rows)
    flat = call(
        functools.partial(finish_kernel, extent_y),
        shape((fields * panels * width // 128, 128), F32),
        [SM] + [VM] * 3,
        VM,
        12,
        flops=2 * panels * fields * width * width,
        moved=8 << 20,
    )(slot, scaled, blocks, returned)
    lanes = width // 128
    leaf_result = flat.reshape(fields, extent_x, lanes, extent_y, 128)
    leaf_result = jnp.transpose(leaf_result, (0, 1, 3, 2, 4)).reshape(voltage.shape)
    return leaf_result, jnp.transpose(result, p_major)


def solution(mesh):
    placed = (
        P(None, "leaf", None, "col"),
        P(None, "leaf", None, "col"),
        P("leaf", None, "col"),
        P("leaf", None, "col", None),
        P("col", "leaf", None, None),
        P("leaf", None, None, "col"),
        P(),
        P(None, "leaf", "col"),
        P("leaf", "col", None),
        P("leaf", "col", None),
    )
    return jax.shard_map(
        level,
        mesh=mesh,
        in_specs=placed,
        out_specs=(P(None, "leaf", None, "col"), P(None, "leaf", "col")),
        check_vma=False,
    )
```

time: 362 us -> 179 us (0.49)
  waiting for transfers between devices: 208 us -> 69.2 us
  matrix products: 29.8 us -> 0 us
  Pallas kernels: 0 us -> 25.9 us
  starting transfers between devices: 66.8 us -> 46.5 us
  between operations: 14.4 us -> 0.98 us
  local copies, waits for them, and re-layouts: 31.4 us -> 23.2 us
    all_gather x1 -> x0, waiting for transfers between devices: 73 us -> none  [body(): shard_piece = lax.all_gather(separator_low, 'leaf', axis=0, tiled=True)]
    ppermute x14 -> x17, waiting for transfers between devices: 85.1 us -> 45.1 us  [shifted(): return lax.ppermute(block, axis, route)]
    dot_general x21 -> x0, matrix products: 29.8 us -> none  [the longest x7 8.05 us: push_up(): return jnp.einsum('eba,enb->ena', coupling, values, precision=highest)]
    all_to_all x2, waiting for transfers between devices: 50.3 us -> 24.1 us  [exchange(): lax.all_to_all(block, 'leaf', split_axis=0, concat_axis=0, tiled=True)]
    pallas_call x0 -> x7, Pallas kernels: none -> 25.9 us  [the longest x1 12.1 us: level(): call(functools.partial(factor_kernel, columns), (square, square), [SM] +...]
    unnamed x27 -> x43, local copies, waits for them, and re-layouts: 4.52 us -> 18.6 us
    ppermute x4 -> x0, starting transfers between devices: 12.3 us -> none  [the longest x2 9.1 us: padded_2(): lax.ppermute(last, axis, up)]
    reshape x6 -> x2, local copies, waits for them, and re-layouts: 8.65 us -> 0.1 us  [the longest x1 0.09 us: level(): targets = update_rows.reshape(entries)]
  transfers between devices with their start and end apart: 21 -> 19, of which waited for: 16 -> 7; matrix products, arithmetic and copies ran while one was open for 7% -> 11% of each run, Pallas kernels for 0% -> 7%
where the time goes in v1:
time: 179 us; the launch traced here: 178 us
  waiting for transfers between devices  69.2 us (39%)
  starting transfers between devices  46.5 us (26%)
  Pallas kernels  25.9 us (14%)
  local copies, waits for them, and re-layouts  23.2 us (13%)
  other arithmetic  12.6 us (7%)
    ppermute x17, waiting for transfers between devices, shifted(): return lax.ppermute(block, axis, route)  45.1 us
    ppermute x17, starting transfers between devices, shifted(): return lax.ppermute(block, axis, route)  30.9 us
    all_to_all x2, waiting for transfers between devices, exchange(): lax.all_to_all(block, 'leaf', split_axis=0, concat_axis=0, tiled=True)  24.1 us
    unnamed x43, local copies, waits for them, and re-layouts  18.6 us
    all_to_all x2, starting transfers between devices, exchange(): lax.all_to_all(block, 'leaf', split_axis=0, concat_axis=0, tiled=True)  15.7 us
    pallas_call x1, Pallas kernels, level(): call(functools.partial(factor_kernel, columns), (square, square), [SM] +...  12.1 us
    convert_element_type x6, other arithmetic, level(): pieces[k] = pieces[k].astype(F32)  8.58 us
    pallas_call x1, Pallas kernels, level(): call(functools.partial(finish_kernel, extent_y), shape((fields * panels *...  4.48 us
  transfers between devices with their start and end apart: 19, of which 7 were waited for; matrix products, arithmetic and copies ran while one was open for 11% of the time, Pallas kernels for 7%

profile of v1, /device:TPU:1, one launch (start us, length us, event | category | flops | bytes accessed | tf_op | source)
XLA Modules:
  0.0 178.4 jit_solution(16702544557745509939)
XLA Ops:
  5.8 2.5 %collective-permute-start.2 = (f16[2,536,256]{2,1,0:T(8,128)(2,1)}, f16[2,536,256]{2,1,0:T(8,128)(2,1)}, u32[]{:S(2)}, u32[]{:S(2)}) collective-permute-start(f16[2,536,256]{2,1,0:T(8,128)(2,1)} %convert_element_type.50), channel_id=1, source_target_pairs={{0,32},{32,64},{64,96},{96,128},{128,160},{160,192},{192,224},{224... | collective-permute-start | bytes 1646600 | tf_op jit(solution)/shard_map/ppermute | solution.py:258
  8.2 3.9 %collective-permute-start.3 = (f16[2,536,256]{2,1,0:T(8,128)(2,1)}, f16[2,536,256]{2,1,0:T(8,128)(2,1)}, u32[]{:S(2)}, u32[]{:S(2)}) collective-permute-start(f16[2,536,256]{2,1,0:T(8,128)(2,1)} %convert_element_type.50), channel_id=1, source_target_pairs={{0,224},{32,0},{64,32},{96,64},{128,96},{160,128},{192,160},{224,1... | collective-permute-start | bytes 1646600 | tf_op jit(solution)/shard_map/ppermute | solution.py:258
  12.2 3.9 %collective-permute-start = (bf16[4,128,256]{2,1,0:T(8,128)(2,1)}, bf16[4,128,256]{2,1,0:T(8,128)(2,1)S(1)}, u32[]{:S(2)}, u32[]{:S(2)}) collective-permute-start(bf16[4,128,256]{2,1,0:T(8,128)(2,1)} %get-tuple-element.13), channel_id=1, source_target_pairs={{0,1},{1,2},{2,3},{3,4},{4,5},{5,6},{6,7},{7,8},{8,9},{9,10},{10,1... | collective-permute-start | bytes 786440 | tf_op jit(solution)/shard_map/ppermute | solution.py:258
  19.0 2.7 %copy.35 = bf16[128,4,4,256]{3,0,2,1:T(8,128)(2,1)} copy(bf16[128,4,4,256]{3,2,1,0:T(4,128)(2,1)} %param.10) | data formatting | bytes 2097152 | tf_op args[0]
  21.8 2.6 %copy.36 = bf16[128,4,4,256]{3,0,2,1:T(8,128)(2,1)} copy(bf16[128,4,4,256]{3,2,1,0:T(4,128)(2,1)} %param.11) | data formatting | bytes 2097152 | tf_op args[1]
  27.2 3.1 %shard_map.114 = (bf16[16,128,256]{2,1,0:T(8,128)(2,1)S(1)}, bf16[32,272,128]{2,1,0:T(8,128)(2,1)S(1)}) custom-call(s32[32]{0:T(128)S(1)} %multiply_add_fusion.slot, bf16[16,128,256]{2,1,0:T(8,128)(2,1)S(1)} %bitcast.42, bf16[16,128,256]{2,1,0:T(8,128)(2,1)S(1)} %bitcast.43, f32[16,256]{1,0:T(8,128)S(1)} %reshape.168.diag, ...), custom_call_target="tpu_custom_call" | custom-call | flops 268435456 | bytes 8388608 | tf_op jit(solution)/shard_map/pallas_call | solution.py:319
  32.7 7.8 %all-to-all-start = ((bf16[32,272,128]{2,1,0:T(8,128)(2,1)}), bf16[32,272,128]{2,1,0:T(8,128)(2,1)S(1)}, u32[]{:S(2)}, u32[]{:S(2)}) async-start(bf16[32,272,128]{2,1,0:T(8,128)(2,1)} %copy-done.7), calls=%async_computation | async-start | bytes 4456448 | tf_op jit(solution)/shard_map/all_to_all | solution.py:351
  40.7 3.4 %collective-permute-start.4 = (f16[2,536,256]{2,1,0:T(8,128)(2,1)}, f16[2,536,256]{2,1,0:T(8,128)(2,1)S(1)}, u32[]{:S(2)}, u32[]{:S(2)}) collective-permute-start(f16[2,536,256]{2,1,0:T(8,128)(2,1)} %collective-permute-done.3), channel_id=1, source_target_pairs={{0,224},{32,0},{64,32},{96,64},{128,96},{160,128},{192,160},{224,1... | collective-permute-start | bytes 1646600 | tf_op jit(solution)/shard_map/ppermute | solution.py:258
  44.1 12.7 %collective-permute-done.6 = f16[2,536,256]{2,1,0:T(8,128)(2,1)S(1)} collective-permute-done((f16[2,536,256]{2,1,0:T(8,128)(2,1)}, f16[2,536,256]{2,1,0:T(8,128)(2,1)S(1)}, u32[]{:S(2)}, u32[]{:S(2)}) %collective-permute-start.6) | collective-permute-done | bytes 548896 | tf_op jit(solution)/shard_map/ppermute | solution.py:258
  56.8 2.7 %collective-permute-start.5 = (f16[2,536,256]{2,1,0:T(8,128)(2,1)S(1)}, f16[2,536,256]{2,1,0:T(8,128)(2,1)S(1)}, u32[]{:S(2)}, u32[]{:S(2)}) collective-permute-start(f16[2,536,256]{2,1,0:T(8,128)(2,1)S(1)} %collective-permute-done.4), channel_id=1, source_target_pairs={{0,224},{32,0},{64,32},{96,64},{128,96},{160,128},{192,160},{224,1... | collective-permute-start | bytes 1646600 | tf_op jit(solution)/shard_map/ppermute | solution.py:258
  59.5 11.7 %collective-permute-done.7 = f16[2,536,256]{2,1,0:T(8,128)(2,1)S(1)} collective-permute-done((f16[2,536,256]{2,1,0:T(8,128)(2,1)S(1)}, f16[2,536,256]{2,1,0:T(8,128)(2,1)S(1)}, u32[]{:S(2)}, u32[]{:S(2)}) %collective-permute-start.7) | collective-permute-done | bytes 548896 | tf_op jit(solution)/shard_map/ppermute | solution.py:258
  71.4 2.9 %collective-permute-start.9 = (f16[1,536,256]{2,1,0:T(8,128)(2,1)S(1)}, f16[1,536,256]{2,1,0:T(8,128)(2,1)S(1)}, u32[]{:S(2)}, u32[]{:S(2)}) collective-permute-start(f16[1,536,256]{2,1,0:T(8,128)(2,1)S(1)} %slice.43), channel_id=1, source_target_pairs={{0,224},{32,0},{64,32},{96,64},{128,96},{160,128},{192,160},{224,1... | collective-permute-start | bytes 823304 | tf_op jit(solution)/shard_map/ppermute | solution.py:258
  75.3 2.1 %convert_element_type.57.refs_1_ = f32[2,536,256]{2,1,0:T(8,128)} convert(f16[2,536,256]{2,1,0:T(8,128)(2,1)} %collective-permute-done.3) | non-fusion elementwise | flops 274432 | bytes 1646592 | tf_op jit(solution)/shard_map/convert_element_type | solution.py:313
  77.4 2.1 %convert_element_type.62.refs_7_ = f32[2,536,256]{2,1,0:T(8,128)} convert(f16[2,536,256]{2,1,0:T(8,128)(2,1)} %collective-permute-done.2) | non-fusion elementwise | flops 274432 | bytes 1646592 | tf_op jit(solution)/shard_map/convert_element_type | solution.py:313
  88.7 12.1 %shard_map.117 = (bf16[8,2,256,256]{3,2,1,0:T(8,128)(2,1)}, bf16[8,2,256,256]{3,2,1,0:T(8,128)(2,1)}) custom-call(s32[1]{0:T(128)} %bitcast.18.place, f32[2,536,256]{2,1,0:T(8,128)} %copy-done.4, f32[2,536,256]{2,1,0:T(8,128)} %convert_element_type.57.refs_1_, f32[2,536,256]{2,1,0:T(8,128)} %convert_element_type.58.refs_2_, ...), custom_call_target="tpu_custom_call" | custom-call | flops 4227858432 | bytes 12582912 | tf_op jit(solution)/shard_map/pallas_call | solution.py:367
  100.9 3.0 %collective-permute-start.13 = (bf16[2,128,256]{2,1,0:T(8,128)(2,1)S(1)}, bf16[2,128,256]{2,1,0:T(8,128)(2,1)S(1)}, u32[]{:S(2)}, u32[]{:S(2)}) collective-permute-start(bf16[2,128,256]{2,1,0:T(8,128)(2,1)S(1)} %get-tuple-element.21.refs_0_), channel_id=1, source_target_pairs={{0,128},{32,160},{64,192},{96,224},{128,0},{160,32},{192,64},{224,... | collective-permute-start | bytes 393224 | tf_op jit(solution)/shard_map/ppermute | solution.py:258
  104.2 2.7 %collective-permute-start.15 = (bf16[2,128,256]{2,1,0:T(8,128)(2,1)S(1)}, bf16[2,128,256]{2,1,0:T(8,128)(2,1)S(1)}, u32[]{:S(2)}, u32[]{:S(2)}) collective-permute-start(bf16[2,128,256]{2,1,0:T(8,128)(2,1)S(1)} %get-tuple-element.21.refs_0_), channel_id=1, source_target_pairs={{0,64},{32,96},{64,128},{96,160},{128,192},{160,224},{192,0},{224,... | collective-permute-start | bytes 393224 | tf_op jit(solution)/shard_map/ppermute | solution.py:258
  110.1 10.0 %collective-permute-done.14.refs_5_ = bf16[2,128,256]{2,1,0:T(8,128)(2,1)S(1)} collective-permute-done((bf16[2,128,256]{2,1,0:T(8,128)(2,1)S(1)}, bf16[2,128,256]{2,1,0:T(8,128)(2,1)S(1)}, u32[]{:S(2)}, u32[]{:S(2)}) %collective-permute-start.14) | collective-permute-done | bytes 131104 | tf_op jit(solution)/shard_map/ppermute | solution.py:258
  120.1 2.6 %collective-permute-done.15.refs_6_ = bf16[2,128,256]{2,1,0:T(8,128)(2,1)S(1)} collective-permute-done((bf16[2,128,256]{2,1,0:T(8,128)(2,1)S(1)}, bf16[2,128,256]{2,1,0:T(8,128)(2,1)S(1)}, u32[]{:S(2)}, u32[]{:S(2)}) %collective-permute-start.15) | collective-permute-done | bytes 131104 | tf_op jit(solution)/shard_map/ppermute | solution.py:258
  122.7 6.3 %collective-permute-done.16.refs_7_ = bf16[2,128,256]{2,1,0:T(8,128)(2,1)S(1)} collective-permute-done((bf16[2,128,256]{2,1,0:T(8,128)(2,1)S(1)}, bf16[2,128,256]{2,1,0:T(8,128)(2,1)S(1)}, u32[]{:S(2)}, u32[]{:S(2)}) %collective-permute-start.16) | collective-permute-done | bytes 131104 | tf_op jit(solution)/shard_map/ppermute | solution.py:258
  132.2 3.6 %shard_map.118 = (f32[2,128,256]{2,1,0:T(8,128)S(1)}, bf16[64,128,128]{2,1,0:T(8,128)(2,1)}) custom-call(s32[64]{0:T(128)S(1)} %convert_element_type.56.tag, bf16[8,2,256,256]{3,2,1,0:T(8,128)(2,1)S(1)} %copy-done.9, bf16[8,2,256,256]{3,2,1,0:T(8,128)(2,1)S(1)} %copy-done.10, bf16[2,128,256]{2,1,0:T(8,128)(2,1)S(1)} %get-tuple-element.21.refs_0_, ...), custom_call_target="tpu_custom_call" | custom-call | flops 536870912 | bytes 8388608 | tf_op jit(solution)/shard_map/pallas_call | solution.py:384
  135.8 7.9 %all-to-all-start.1 = ((bf16[32,2,128,128]{3,2,1,0:T(8,128)(2,1)}), bf16[32,2,128,128]{3,2,1,0:T(8,128)(2,1)}, u32[]{:S(2)}, u32[]{:S(2)}) async-start(bf16[32,2,128,128]{3,2,1,0:T(8,128)(2,1)} %bitcast.19), calls=%async_computation.1 | async-start | bytes 4194304 | tf_op jit(solution)/shard_map/all_to_all | solution.py:351
  148.3 24.1 %all-to-all-done.1 = bf16[32,2,128,128]{3,2,1,0:T(8,128)(2,1)} async-done(((bf16[32,2,128,128]{3,2,1,0:T(8,128)(2,1)}), bf16[32,2,128,128]{3,2,1,0:T(8,128)(2,1)}, u32[]{:S(2)}, u32[]{:S(2)}) %all-to-all-start.1) | async-done | bytes 2097184 | tf_op jit(solution)/shard_map/all_to_all | solution.py:351
  174.0 4.5 %shard_map.119 = f32[4096,128]{1,0:T(8,128)} custom-call(s32[32]{0:T(128)S(1)} %multiply_add_fusion.slot, f32[16,128,256]{2,1,0:T(8,128)S(1)} %copy-done.3, bf16[16,256,256]{2,1,0:T(8,128)(2,1)S(1)} %bitcast.41, bf16[64,128,128]{2,1,0:T(8,128)(2,1)} %bitcast.20.received), custom_call_target="tpu_custom_call" | custom-call | flops 268435456 | bytes 8388608 | tf_op jit(solution)/shard_map/pallas_call | solution.py:395
  (98 shorter events, 36.4 us)
Async XLA Ops:
  3.6 14.4 %copy-start.17 = (s32[1,4,4,2]{2,3,1,0:T(2,128)S(1)}, s32[1,4,4,2]{2,3,1,0:T(2,128)}, u32[]{:S(2)}) copy-start(s32[1,4,4,2]{2,3,1,0:T(2,128)} %param.14) | copy-start | bytes 388
  3.6 14.7 %copy-start.18 = (s32[64]{0:T(128)S(1)}, s32[64]{0:T(128)}, u32[]{:S(2)}) copy-start(s32[64]{0:T(128)} %param.16) | copy-start | bytes 772
  3.9 17.9 %copy-start.4 = (f32[2,536,256]{2,1,0:T(8,128)}, f32[2,536,256]{2,1,0:T(8,128)S(1)}, u32[]{:S(2)}) copy-start(f32[2,536,256]{2,1,0:T(8,128)S(1)} %shard_map.113.refs_0_) | copy-start | bytes 3293188
  5.8 19.4 %collective-permute-start.2 = (f16[2,536,256]{2,1,0:T(8,128)(2,1)}, f16[2,536,256]{2,1,0:T(8,128)(2,1)}, u32[]{:S(2)}, u32[]{:S(2)}) collective-permute-start(f16[2,536,256]{2,1,0:T(8,128)(2,1)} %convert_element_type.50), channel_id=1, source_target_pairs={{0,32},{32,64},{64,96},{96,128},{128,160},{160,192},{192,224},{224... | collective-permute-start | bytes 1646600 | tf_op jit(solution)/shard_map/ppermute | solution.py:258
  8.2 16.2 %collective-permute-start.3 = (f16[2,536,256]{2,1,0:T(8,128)(2,1)}, f16[2,536,256]{2,1,0:T(8,128)(2,1)}, u32[]{:S(2)}, u32[]{:S(2)}) collective-permute-start(f16[2,536,256]{2,1,0:T(8,128)(2,1)} %convert_element_type.50), channel_id=1, source_target_pairs={{0,224},{32,0},{64,32},{96,64},{128,96},{160,128},{192,160},{224,1... | collective-permute-start | bytes 1646600 | tf_op jit(solution)/shard_map/ppermute | solution.py:258
  12.2 13.7 %collective-permute-start = (bf16[4,128,256]{2,1,0:T(8,128)(2,1)}, bf16[4,128,256]{2,1,0:T(8,128)(2,1)S(1)}, u32[]{:S(2)}, u32[]{:S(2)}) collective-permute-start(bf16[4,128,256]{2,1,0:T(8,128)(2,1)} %get-tuple-element.13), channel_id=1, source_target_pairs={{0,1},{1,2},{2,3},{3,4},{4,5},{5,6},{6,7},{7,8},{8,9},{9,10},{10,1... | collective-permute-start | bytes 786440 | tf_op jit(solution)/shard_map/ppermute | solution.py:258
  16.1 9.7 %collective-permute-start.1 = (bf16[4,128,256]{2,1,0:T(8,128)(2,1)}, bf16[4,128,256]{2,1,0:T(8,128)(2,1)}, u32[]{:S(2)}, u32[]{:S(2)}) collective-permute-start(bf16[4,128,256]{2,1,0:T(8,128)(2,1)} %get-tuple-element.14), channel_id=1, source_target_pairs={{1,0},{2,1},{3,2},{4,3},{5,4},{6,5},{7,6},{8,7},{9,8},{10,9},{11,1... | collective-permute-start | bytes 786440 | tf_op jit(solution)/shard_map/ppermute | solution.py:258
  32.7 52.3 %all-to-all-start = ((bf16[32,272,128]{2,1,0:T(8,128)(2,1)}), bf16[32,272,128]{2,1,0:T(8,128)(2,1)S(1)}, u32[]{:S(2)}, u32[]{:S(2)}) async-start(bf16[32,272,128]{2,1,0:T(8,128)(2,1)} %copy-done.7), calls=%async_computation | async-start | bytes 4456448 | tf_op jit(solution)/shard_map/all_to_all | solution.py:351
  40.6 16.2 %collective-permute-start.6 = (f16[2,536,256]{2,1,0:T(8,128)(2,1)}, f16[2,536,256]{2,1,0:T(8,128)(2,1)S(1)}, u32[]{:S(2)}, u32[]{:S(2)}) collective-permute-start(f16[2,536,256]{2,1,0:T(8,128)(2,1)} %collective-permute-done.2), channel_id=1, source_target_pairs={{0,32},{32,64},{64,96},{96,128},{128,160},{160,192},{192,224},{224... | collective-permute-start | bytes 1646600 | tf_op jit(solution)/shard_map/ppermute | solution.py:258
  40.7 16.1 %collective-permute-start.4 = (f16[2,536,256]{2,1,0:T(8,128)(2,1)}, f16[2,536,256]{2,1,0:T(8,128)(2,1)S(1)}, u32[]{:S(2)}, u32[]{:S(2)}) collective-permute-start(f16[2,536,256]{2,1,0:T(8,128)(2,1)} %collective-permute-done.3), channel_id=1, source_target_pairs={{0,224},{32,0},{64,32},{96,64},{128,96},{160,128},{192,160},{224,1... | collective-permute-start | bytes 1646600 | tf_op jit(solution)/shard_map/ppermute | solution.py:258
  56.8 14.4 %collective-permute-start.7 = (f16[2,536,256]{2,1,0:T(8,128)(2,1)S(1)}, f16[2,536,256]{2,1,0:T(8,128)(2,1)S(1)}, u32[]{:S(2)}, u32[]{:S(2)}) collective-permute-start(f16[2,536,256]{2,1,0:T(8,128)(2,1)S(1)} %collective-permute-done.6), channel_id=1, source_target_pairs={{0,32},{32,64},{64,96},{96,128},{128,160},{160,192},{192,224},{224... | collective-permute-start | bytes 1646600 | tf_op jit(solution)/shard_map/ppermute | solution.py:258
  56.8 14.6 %collective-permute-start.5 = (f16[2,536,256]{2,1,0:T(8,128)(2,1)S(1)}, f16[2,536,256]{2,1,0:T(8,128)(2,1)S(1)}, u32[]{:S(2)}, u32[]{:S(2)}) collective-permute-start(f16[2,536,256]{2,1,0:T(8,128)(2,1)S(1)} %collective-permute-done.4), channel_id=1, source_target_pairs={{0,224},{32,0},{64,32},{96,64},{128,96},{160,128},{192,160},{224,1... | collective-permute-start | bytes 1646600 | tf_op jit(solution)/shard_map/ppermute | solution.py:258
  71.3 12.6 %collective-permute-start.8 = (f16[1,536,256]{2,1,0:T(8,128)(2,1)S(1)}, f16[1,536,256]{2,1,0:T(8,128)(2,1)S(1)}, u32[]{:S(2)}, u32[]{:S(2)}) collective-permute-start(f16[1,536,256]{2,1,0:T(8,128)(2,1)S(1)} %slice.42), channel_id=1, source_target_pairs={{0,32},{32,64},{64,96},{96,128},{128,160},{160,192},{192,224},{224... | collective-permute-start | bytes 823304 | tf_op jit(solution)/shard_map/ppermute | solution.py:258
  71.4 12.5 %collective-permute-start.9 = (f16[1,536,256]{2,1,0:T(8,128)(2,1)S(1)}, f16[1,536,256]{2,1,0:T(8,128)(2,1)S(1)}, u32[]{:S(2)}, u32[]{:S(2)}) collective-permute-start(f16[1,536,256]{2,1,0:T(8,128)(2,1)S(1)} %slice.43), channel_id=1, source_target_pairs={{0,224},{32,0},{64,32},{96,64},{128,96},{160,128},{192,160},{224,1... | collective-permute-start | bytes 823304 | tf_op jit(solution)/shard_map/ppermute | solution.py:258
  86.7 17.5 %collective-permute-start.10 = (bf16[2,128,256]{2,1,0:T(8,128)(2,1)S(1)}, bf16[2,128,256]{2,1,0:T(8,128)(2,1)S(1)}, u32[]{:S(2)}, u32[]{:S(2)}) collective-permute-start(bf16[2,128,256]{2,1,0:T(8,128)(2,1)S(1)} %get-tuple-element.21.refs_0_), channel_id=1, source_target_pairs={{0,224},{32,0},{64,32},{96,64},{128,96},{160,128},{192,160},{224,1... | collective-permute-start | bytes 393224 | tf_op jit(solution)/shard_map/ppermute | solution.py:258
  86.8 20.1 %collective-permute-start.11 = (bf16[2,128,256]{2,1,0:T(8,128)(2,1)S(1)}, bf16[2,128,256]{2,1,0:T(8,128)(2,1)S(1)}, u32[]{:S(2)}, u32[]{:S(2)}) collective-permute-start(bf16[2,128,256]{2,1,0:T(8,128)(2,1)S(1)} %get-tuple-element.21.refs_0_), channel_id=1, source_target_pairs={{0,192},{32,224},{64,0},{96,32},{128,64},{160,96},{192,128},{224,1... | collective-permute-start | bytes 393224 | tf_op jit(solution)/shard_map/ppermute | solution.py:258
  100.8 9.2 %collective-permute-start.12 = (bf16[2,128,256]{2,1,0:T(8,128)(2,1)S(1)}, bf16[2,128,256]{2,1,0:T(8,128)(2,1)S(1)}, u32[]{:S(2)}, u32[]{:S(2)}) collective-permute-start(bf16[2,128,256]{2,1,0:T(8,128)(2,1)S(1)} %get-tuple-element.21.refs_0_), channel_id=1, source_target_pairs={{0,160},{32,192},{64,224},{96,0},{128,32},{160,64},{192,96},{224,1... | collective-permute-start | bytes 393224 | tf_op jit(solution)/shard_map/ppermute | solution.py:258
  100.9 9.2 %collective-permute-start.13 = (bf16[2,128,256]{2,1,0:T(8,128)(2,1)S(1)}, bf16[2,128,256]{2,1,0:T(8,128)(2,1)S(1)}, u32[]{:S(2)}, u32[]{:S(2)}) collective-permute-start(bf16[2,128,256]{2,1,0:T(8,128)(2,1)S(1)} %get-tuple-element.21.refs_0_), channel_id=1, source_target_pairs={{0,128},{32,160},{64,192},{96,224},{128,0},{160,32},{192,64},{224,... | collective-permute-start | bytes 393224 | tf_op jit(solution)/shard_map/ppermute | solution.py:258
  103.9 16.2 %collective-permute-start.14 = (bf16[2,128,256]{2,1,0:T(8,128)(2,1)S(1)}, bf16[2,128,256]{2,1,0:T(8,128)(2,1)S(1)}, u32[]{:S(2)}, u32[]{:S(2)}) collective-permute-start(bf16[2,128,256]{2,1,0:T(8,128)(2,1)S(1)} %get-tuple-element.21.refs_0_), channel_id=1, source_target_pairs={{0,96},{32,128},{64,160},{96,192},{128,224},{160,0},{192,32},{224,... | collective-permute-start | bytes 393224 | tf_op jit(solution)/shard_map/ppermute | solution.py:258
  104.2 18.5 %collective-permute-start.15 = (bf16[2,128,256]{2,1,0:T(8,128)(2,1)S(1)}, bf16[2,128,256]{2,1,0:T(8,128)(2,1)S(1)}, u32[]{:S(2)}, u32[]{:S(2)}) collective-permute-start(bf16[2,128,256]{2,1,0:T(8,128)(2,1)S(1)} %get-tuple-element.21.refs_0_), channel_id=1, source_target_pairs={{0,64},{32,96},{64,128},{96,160},{128,192},{160,224},{192,0},{224,... | collective-permute-start | bytes 393224 | tf_op jit(solution)/shard_map/ppermute | solution.py:258
  106.9 22.1 %collective-permute-start.16 = (bf16[2,128,256]{2,1,0:T(8,128)(2,1)S(1)}, bf16[2,128,256]{2,1,0:T(8,128)(2,1)S(1)}, u32[]{:S(2)}, u32[]{:S(2)}) collective-permute-start(bf16[2,128,256]{2,1,0:T(8,128)(2,1)S(1)} %get-tuple-element.21.refs_0_), channel_id=1, source_target_pairs={{0,32},{32,64},{64,96},{96,128},{128,160},{160,192},{192,224},{224... | collective-permute-start | bytes 393224 | tf_op jit(solution)/shard_map/ppermute | solution.py:258
  135.8 7.9 %copy-start.12 = (bf16[16,128,256]{2,1,0:T(8,128)(2,1)S(1)}, bf16[16,128,256]{2,1,0:T(8,128)(2,1)}, u32[]{:S(2)}) copy-start(bf16[16,128,256]{2,1,0:T(8,128)(2,1)} %copy-done.11) | copy-start | bytes 3145732
  135.8 36.6 %all-to-all-start.1 = ((bf16[32,2,128,128]{3,2,1,0:T(8,128)(2,1)}), bf16[32,2,128,128]{3,2,1,0:T(8,128)(2,1)}, u32[]{:S(2)}, u32[]{:S(2)}) async-start(bf16[32,2,128,128]{3,2,1,0:T(8,128)(2,1)} %bitcast.19), calls=%async_computation.1 | async-start | bytes 4194304 | tf_op jit(solution)/shard_map/all_to_all | solution.py:351
  145.2 27.1 %copy-start.1 = (bf16[4,4,256,256]{3,2,1,0:T(8,128)(2,1)S(1)}, bf16[4,4,256,256]{3,2,1,0:T(8,128)(2,1)}, u32[]{:S(2)}) copy-start(bf16[4,4,256,256]{3,2,1,0:T(8,128)(2,1)} %param.15) | copy-start | bytes 6291460
  (14 other events, 35.8 us)

commit v2 on v1

--- a/solution.py
+++ b/solution.py
@@ -12,7 +12,7 @@
 F32 = jnp.float32
 BF16 = jnp.bfloat16
 MIB = 1 << 20
-FACTOR_MIB = 56
+FACTOR_MIB = 24
 
 
 def dot(a, b, kind):
@@ -80,13 +80,13 @@
     step = 32
 
     def mark(s, r):
-        return received[s, capacity * fields : capacity * fields + 16, :].astype(F32)[8 * r : 8 * r + 8]
+        return received[s, capacity * fields : capacity * fields + 8, :].astype(F32)[r : r + 1]
 
     lane = lax.broadcasted_iota(jnp.int32, (1, rows), 1)
     for s in range(owners):
-        line = mark(s, 0)[:1]
+        line = mark(s, 0)
         for r in range(1, capacity):
-            line = jnp.where(lane == r, mark(s, r)[:1], line)
+            line = jnp.where(lane == r, mark(s, r), line)
         tags[s : s + 1, :] = line
     for c in range(fields // step):
         span = slice(c * step, (c + 1) * step)
@@ -97,7 +97,7 @@
         def add(s, totals):
             totals = list(totals)
             for r in range(capacity):
-                tag = jnp.concatenate([mark(s, r)] * (step // 8), axis=0)
+                tag = jnp.broadcast_to(mark(s, r), (step, rows))
                 start = r * fields + c * step
                 block = received[s, start : start + step, :].astype(F32)
                 for b in range(count):
@@ -200,18 +200,29 @@
     lax.fori_loop(0, sent.shape[0], pick, 0, unroll=4)
 
 
-def finish_kernel(extent_y, slot, scaled, blocks, received, out):
-    panels, fields, width = scaled.shape
-    lanes = width // 128
-    group = out.shape[0] // fields
+def finish_kernel(extent_y, slot, scaled_in, blocks_in, received, out, scaled, blocks, picks, sems, pick_sems):
+    panels = scaled.shape[0]
     per_leaf = slot.shape[0] // panels
+    loads = []
+    for g in range(panels // extent_y):
+        part = pl.ds(g * extent_y, extent_y)
+        load = [
+            pltpu.make_async_copy(blocks_in.at[part], blocks.at[part], sems.at[2 * g]),
+            pltpu.make_async_copy(scaled_in.at[part], scaled.at[part], sems.at[2 * g + 1]),
+        ]
+        for e in range(g * extent_y * per_leaf, (g + 1) * extent_y * per_leaf):
+            load.append(pltpu.make_async_copy(received.at[slot[e]], picks.at[e], pick_sems.at[e]))
+        for copy in load:
+            copy.start()
+        loads.append(load)
     for p in range(panels):
-        picked = [received[slot[p * per_leaf + k]] for k in range(per_leaf)]
+        x, y = divmod(p, extent_y)
+        if y == 0:
+            for copy in loads[x]:
+                copy.wait()
+        picked = [picks[p * per_leaf + k] for k in range(per_leaf)]
         acc = scaled[p] - dot(jnp.concatenate(picked, axis=1), blocks[p], "nn")
-        x, y = divmod(p, extent_y)
-        for part in range(lanes):
-            start = (x * lanes + part) * extent_y + y
-            out[pl.ds(start, fields, stride=group), :] = acc[:, part * 128 : (part + 1) * 128]
+        out[:, x, y, :] = acc
 
 
 def call(kernel, out_shape, in_specs, out_specs, limit, scratch=(), flops=0, moved=0):
@@ -290,8 +301,8 @@
     slot = owner * capacity + jnp.sum(same.astype(jnp.int32), axis=1)
     slot_hit = slot[:, None] == jnp.arange(slots, dtype=jnp.int32)[None, :]
     out_tags = jnp.sum(jnp.where(slot_hit, local[:, None] + 1, 0), axis=0) - 1
-    marks = jnp.broadcast_to(out_tags.astype(BF16).reshape(owners, capacity, 1, 1), (owners, capacity, 8, rows))
-    marks = marks.reshape(owners, capacity * 8, rows)
+    marks = jnp.pad(out_tags.astype(BF16).reshape(owners, capacity, 1), ((0, 0), (0, 8 - capacity), (0, 0)))
+    marks = jnp.broadcast_to(marks, (owners, 8, rows))
 
     pieces = [padded] + [None] * (columns - 1)
     up = down = packed
@@ -318,7 +329,7 @@
     p_major = (1, 0, 2)
     low, sent = call(
         functools.partial(leaf_kernel, extent_y),
-        (shape((panels, fields, width), BF16), shape((owners, capacity * fields + 16, rows), BF16)),
+        (shape((panels, fields, width), BF16), shape((owners, capacity * fields + 8, rows), BF16)),
         [SM] + [VM] * 9,
         (VM, VM),
         12,
@@ -380,7 +391,9 @@
         moved=12 << 20,
     )(place, *pieces)
 
-    drives = [drive] + [shifted(drive, "col", -k, True) for k in range(1, columns)]
+    drives = [drive] * columns
+    for k in sorted(range(1, columns), key=lambda k: -min(k, columns - k)):
+        drives[k] = shifted(drive, "col", -k, True)
     result, answer = call(
         functools.partial(solve_kernel, columns),
         (shape((sep_rows, fields, width), F32), shape((slots, fields, rows), BF16)),
@@ -392,18 +405,22 @@
         moved=8 << 20,
     )(in_tags, m_high, m_low, *drives)
     returned = exchange(answer.reshape(owners, capacity, fields, rows)).reshape(slots, fields, rows)
-    flat = call(
+    leaf_result = call(
         functools.partial(finish_kernel, extent_y),
-        shape((fields * panels * width // 128, 128), F32),
-        [SM] + [VM] * 3,
+        shape(voltage.shape, F32),
+        [SM] + [HB] * 3,
         VM,
-        12,
+        56,
+        scratch=[
+            pltpu.VMEM((panels, fields, width), F32),
+            pltpu.VMEM((panels, per_leaf * rows, width), BF16),
+            pltpu.VMEM((entries, fields, rows), BF16),
+            pltpu.SemaphoreType.DMA((2 * extent_x,)),
+            pltpu.SemaphoreType.DMA((entries,)),
+        ],
         flops=2 * panels * fields * width * width,
         moved=8 << 20,
     )(slot, scaled, blocks, returned)
-    lanes = width // 128
-    leaf_result = flat.reshape(fields, extent_x, lanes, extent_y, 128)
-    leaf_result = jnp.transpose(leaf_result, (0, 1, 3, 2, 4)).reshape(voltage.shape)
     return leaf_result, jnp.transpose(result, p_major)
 
 

time: 179 us -> 185 us (1.034)
  local copies, waits for them, and re-layouts: 23.2 us -> 29 us
  waiting for transfers between devices: 69.2 us -> 72.3 us
    unnamed x43 -> x63, local copies, waits for them, and re-layouts: 18.6 us -> 24 us
    pallas_call x1, Pallas kernels: 12.1 us -> 9.8 us  [level(): call(functools.partial(factor_kernel, columns), (square, square), [SM] +...]
  transfers between devices with their start and end apart: 19 -> 19, of which waited for: 7 -> 8; matrix products, arithmetic and copies ran while one was open for 11% -> 10% of each run, Pallas kernels for 7% -> 6%
where the time goes in v2:
time: 185 us; the launch traced here: 184 us
  waiting for transfers between devices  72.3 us (39%)
  starting transfers between devices  45.1 us (24%)
  local copies, waits for them, and re-layouts  29 us (16%)
  Pallas kernels  24.3 us (13%)
  other arithmetic  12.5 us (7%)
    ppermute x17, waiting for transfers between devices, shifted(): return lax.ppermute(block, axis, route)  46.6 us
    ppermute x17, starting transfers between devices, shifted(): return lax.ppermute(block, axis, route)  29 us
    all_to_all x2, waiting for transfers between devices, exchange(): lax.all_to_all(block, 'leaf', split_axis=0, concat_axis=0, tiled=True)  25.7 us
    unnamed x63, local copies, waits for them, and re-layouts  24 us
    all_to_all x2, starting transfers between devices, exchange(): lax.all_to_all(block, 'leaf', split_axis=0, concat_axis=0, tiled=True)  16.1 us
    pallas_call x1, Pallas kernels, level(): call(functools.partial(factor_kernel, columns), (square, square), [SM] +...  9.8 us
    convert_element_type x6, other arithmetic, level(): pieces[k] = pieces[k].astype(F32)  8.66 us
    pallas_call x1, Pallas kernels, level(): call(functools.partial(finish_kernel, extent_y), shape(voltage.shape, F32...  5.4 us
  transfers between devices with their start and end apart: 19, of which 8 were waited for; matrix products, arithmetic and copies ran while one was open for 10% of the time, Pallas kernels for 6%

profile of v2, /device:TPU:1, one launch (start us, length us, event | category | flops | bytes accessed | tf_op | source)
XLA Modules:
  0.0 184.4 jit_solution(7357507781140188438)
XLA Ops:
  6.3 2.5 %collective-permute-start.2 = (f16[2,536,256]{2,1,0:T(8,128)(2,1)}, f16[2,536,256]{2,1,0:T(8,128)(2,1)}, u32[]{:S(2)}, u32[]{:S(2)}) collective-permute-start(f16[2,536,256]{2,1,0:T(8,128)(2,1)} %convert_element_type.55), channel_id=1, source_target_pairs={{0,32},{32,64},{64,96},{96,128},{128,160},{160,192},{192,224},{224... | collective-permute-start | bytes 1646600 | tf_op jit(solution)/shard_map/ppermute | solution.py:269
  8.8 3.9 %collective-permute-start.3 = (f16[2,536,256]{2,1,0:T(8,128)(2,1)}, f16[2,536,256]{2,1,0:T(8,128)(2,1)}, u32[]{:S(2)}, u32[]{:S(2)}) collective-permute-start(f16[2,536,256]{2,1,0:T(8,128)(2,1)} %convert_element_type.55), channel_id=1, source_target_pairs={{0,224},{32,0},{64,32},{96,64},{128,96},{160,128},{192,160},{224,1... | collective-permute-start | bytes 1646600 | tf_op jit(solution)/shard_map/ppermute | solution.py:269
  12.7 3.9 %collective-permute-start = (bf16[4,128,256]{2,1,0:T(8,128)(2,1)}, bf16[4,128,256]{2,1,0:T(8,128)(2,1)S(1)}, u32[]{:S(2)}, u32[]{:S(2)}) collective-permute-start(bf16[4,128,256]{2,1,0:T(8,128)(2,1)} %get-tuple-element.13), channel_id=1, source_target_pairs={{0,1},{1,2},{2,3},{3,4},{4,5},{5,6},{6,7},{7,8},{8,9},{9,10},{10,1... | collective-permute-start | bytes 786440 | tf_op jit(solution)/shard_map/ppermute | solution.py:269
  16.7 1.9 %collective-permute-start.1 = (bf16[4,128,256]{2,1,0:T(8,128)(2,1)}, bf16[4,128,256]{2,1,0:T(8,128)(2,1)}, u32[]{:S(2)}, u32[]{:S(2)}) collective-permute-start(bf16[4,128,256]{2,1,0:T(8,128)(2,1)} %get-tuple-element.14), channel_id=1, source_target_pairs={{1,0},{2,1},{3,2},{4,3},{5,4},{6,5},{7,6},{8,7},{9,8},{10,9},{11,1... | collective-permute-start | bytes 786440 | tf_op jit(solution)/shard_map/ppermute | solution.py:269
  20.8 2.6 %copy.32 = bf16[128,4,4,256]{3,0,2,1:T(8,128)(2,1)} copy(bf16[128,4,4,256]{3,2,1,0:T(4,128)(2,1)} %param.11) | data formatting | bytes 2097152 | tf_op args[1]
  28.5 3.3 %shard_map.114 = (bf16[16,128,256]{2,1,0:T(8,128)(2,1)S(1)}, bf16[32,264,128]{2,1,0:T(8,128)(2,1)S(1)}) custom-call(s32[32]{0:T(128)S(1)} %multiply_add_fusion.slot, bf16[16,128,256]{2,1,0:T(8,128)(2,1)S(1)} %bitcast.37, bf16[16,128,256]{2,1,0:T(8,128)(2,1)S(1)} %bitcast.38, f32[16,256]{1,0:T(8,128)S(1)} %reshape.167.diag, ...), custom_call_target="tpu_custom_call" | custom-call | flops 268435456 | bytes 8388608 | tf_op jit(solution)/shard_map/pallas_call | solution.py:330
  34.0 8.3 %all-to-all-start = ((bf16[32,264,128]{2,1,0:T(8,128)(2,1)}), bf16[32,264,128]{2,1,0:T(8,128)(2,1)S(1)}, u32[]{:S(2)}, u32[]{:S(2)}) async-start(bf16[32,264,128]{2,1,0:T(8,128)(2,1)} %copy-done.4), calls=%async_computation | async-start | bytes 4325376 | tf_op jit(solution)/shard_map/all_to_all | solution.py:362
  42.5 3.4 %collective-permute-start.4 = (f16[2,536,256]{2,1,0:T(8,128)(2,1)}, f16[2,536,256]{2,1,0:T(8,128)(2,1)S(1)}, u32[]{:S(2)}, u32[]{:S(2)}) collective-permute-start(f16[2,536,256]{2,1,0:T(8,128)(2,1)} %collective-permute-done.3), channel_id=1, source_target_pairs={{0,224},{32,0},{64,32},{96,64},{128,96},{160,128},{192,160},{224,1... | collective-permute-start | bytes 1646600 | tf_op jit(solution)/shard_map/ppermute | solution.py:269
  45.9 12.7 %collective-permute-done.6 = f16[2,536,256]{2,1,0:T(8,128)(2,1)S(1)} collective-permute-done((f16[2,536,256]{2,1,0:T(8,128)(2,1)}, f16[2,536,256]{2,1,0:T(8,128)(2,1)S(1)}, u32[]{:S(2)}, u32[]{:S(2)}) %collective-permute-start.6) | collective-permute-done | bytes 548896 | tf_op jit(solution)/shard_map/ppermute | solution.py:269
  58.6 2.7 %collective-permute-start.5 = (f16[2,536,256]{2,1,0:T(8,128)(2,1)S(1)}, f16[2,536,256]{2,1,0:T(8,128)(2,1)S(1)}, u32[]{:S(2)}, u32[]{:S(2)}) collective-permute-start(f16[2,536,256]{2,1,0:T(8,128)(2,1)S(1)} %collective-permute-done.4), channel_id=1, source_target_pairs={{0,224},{32,0},{64,32},{96,64},{128,96},{160,128},{192,160},{224,1... | collective-permute-start | bytes 1646600 | tf_op jit(solution)/shard_map/ppermute | solution.py:269
  61.3 11.7 %collective-permute-done.7 = f16[2,536,256]{2,1,0:T(8,128)(2,1)S(1)} collective-permute-done((f16[2,536,256]{2,1,0:T(8,128)(2,1)S(1)}, f16[2,536,256]{2,1,0:T(8,128)(2,1)S(1)}, u32[]{:S(2)}, u32[]{:S(2)}) %collective-permute-start.7) | collective-permute-done | bytes 548896 | tf_op jit(solution)/shard_map/ppermute | solution.py:269
  73.2 2.9 %collective-permute-start.9 = (f16[1,536,256]{2,1,0:T(8,128)(2,1)S(1)}, f16[1,536,256]{2,1,0:T(8,128)(2,1)S(1)}, u32[]{:S(2)}, u32[]{:S(2)}) collective-permute-start(f16[1,536,256]{2,1,0:T(8,128)(2,1)S(1)} %slice.43), channel_id=1, source_target_pairs={{0,224},{32,0},{64,32},{96,64},{128,96},{160,128},{192,160},{224,1... | collective-permute-start | bytes 823304 | tf_op jit(solution)/shard_map/ppermute | solution.py:269
  77.1 2.1 %convert_element_type.62.refs_1_ = f32[2,536,256]{2,1,0:T(8,128)} convert(f16[2,536,256]{2,1,0:T(8,128)(2,1)} %collective-permute-done.3) | non-fusion elementwise | flops 274432 | bytes 1646592 | tf_op jit(solution)/shard_map/convert_element_type | solution.py:324
  79.2 2.1 %convert_element_type.67.refs_7_ = f32[2,536,256]{2,1,0:T(8,128)} convert(f16[2,536,256]{2,1,0:T(8,128)(2,1)} %collective-permute-done.2) | non-fusion elementwise | flops 274432 | bytes 1646592 | tf_op jit(solution)/shard_map/convert_element_type | solution.py:324
  86.9 2.3 %shard_map.116 = (bf16[2,128,256]{2,1,0:T(8,128)(2,1)}, f32[32,128]{1,0:T(8,128)S(1)}) custom-call(bf16[32,264,128]{2,1,0:T(8,128)(2,1)S(1)} %all-to-all-done.received, f32[2,128,256]{2,1,0:T(8,128)S(1)} %bitcast.41), custom_call_target="tpu_custom_call" | custom-call | flops 1048576 | bytes 3145728 | tf_op jit(solution)/shard_map/pallas_call | solution.py:365
  97.3 9.8 %shard_map.117 = (bf16[8,2,256,256]{3,2,1,0:T(8,128)(2,1)S(1)}, bf16[8,2,256,256]{3,2,1,0:T(8,128)(2,1)S(1)}) custom-call(s32[1]{0:T(128)} %bitcast.18.place, f32[2,536,256]{2,1,0:T(8,128)S(1)} %shard_map.113.refs_0_, f32[2,536,256]{2,1,0:T(8,128)S(1)} %copy-done.9, f32[2,536,256]{2,1,0:T(8,128)S(1)} %copy-done.11, f32[2,536,256]{2,1,0:T(8,128)S(1)} %copy-done.13, ...), custom_call_target="tpu_custom_call" | custom-call | flops 4227858432 | bytes 12582912 | tf_op jit(solution)/shard_map/pallas_call | solution.py:378
  108.4 3.0 %collective-permute-start.13 = (bf16[2,128,256]{2,1,0:T(8,128)(2,1)}, bf16[2,128,256]{2,1,0:T(8,128)(2,1)S(1)}, u32[]{:S(2)}, u32[]{:S(2)}) collective-permute-start(bf16[2,128,256]{2,1,0:T(8,128)(2,1)} %get-tuple-element.21.refs_0_), channel_id=1, source_target_pairs={{0,128},{32,160},{64,192},{96,224},{128,0},{160,32},{192,64},{224,... | collective-permute-start | bytes 393224 | tf_op jit(solution)/shard_map/ppermute | solution.py:269
  114.9 4.6 %collective-permute-done.12.refs_3_ = bf16[2,128,256]{2,1,0:T(8,128)(2,1)S(1)} collective-permute-done((bf16[2,128,256]{2,1,0:T(8,128)(2,1)}, bf16[2,128,256]{2,1,0:T(8,128)(2,1)S(1)}, u32[]{:S(2)}, u32[]{:S(2)}) %collective-permute-start.12) | collective-permute-done | bytes 131104 | tf_op jit(solution)/shard_map/ppermute | solution.py:269
  119.5 9.6 %collective-permute-done.14.refs_5_ = bf16[2,128,256]{2,1,0:T(8,128)(2,1)S(1)} collective-permute-done((bf16[2,128,256]{2,1,0:T(8,128)(2,1)}, bf16[2,128,256]{2,1,0:T(8,128)(2,1)S(1)}, u32[]{:S(2)}, u32[]{:S(2)}) %collective-permute-start.14) | collective-permute-done | bytes 131104 | tf_op jit(solution)/shard_map/ppermute | solution.py:269
  129.1 6.8 %collective-permute-done.16.refs_7_ = bf16[2,128,256]{2,1,0:T(8,128)(2,1)S(1)} collective-permute-done((bf16[2,128,256]{2,1,0:T(8,128)(2,1)}, bf16[2,128,256]{2,1,0:T(8,128)(2,1)S(1)}, u32[]{:S(2)}, u32[]{:S(2)}) %collective-permute-start.16) | collective-permute-done | bytes 131104 | tf_op jit(solution)/shard_map/ppermute | solution.py:269
  138.4 2.6 %shard_map.118 = (f32[2,128,256]{2,1,0:T(8,128)S(1)}, bf16[64,128,128]{2,1,0:T(8,128)(2,1)S(1)}) custom-call(s32[64]{0:T(128)S(1)} %convert_element_type.61.tag, bf16[8,2,256,256]{3,2,1,0:T(8,128)(2,1)S(1)} %get-tuple-element.19.m_high, bf16[8,2,256,256]{3,2,1,0:T(8,128)(2,1)S(1)} %copy-done.7, bf16[2,128,256]{2,1,0:T(8,128)(2,1)} %get-tuple-element.21.refs_0_, ...), custom_call_target="tpu_custom_call" | custom-call | flops 536870912 | bytes 8388608 | tf_op jit(solution)/shard_map/pallas_call | solution.py:397
  142.3 7.8 %all-to-all-start.1 = ((bf16[32,2,128,128]{3,2,1,0:T(8,128)(2,1)}), bf16[32,2,128,128]{3,2,1,0:T(8,128)(2,1)}, u32[]{:S(2)}, u32[]{:S(2)}) async-start(bf16[32,2,128,128]{3,2,1,0:T(8,128)(2,1)} %bitcast.40), calls=%async_computation.1 | async-start | bytes 4194304 | tf_op jit(solution)/shard_map/all_to_all | solution.py:362
  153.2 25.7 %all-to-all-done.1 = bf16[32,2,128,128]{3,2,1,0:T(8,128)(2,1)} async-done(((bf16[32,2,128,128]{3,2,1,0:T(8,128)(2,1)}), bf16[32,2,128,128]{3,2,1,0:T(8,128)(2,1)}, u32[]{:S(2)}, u32[]{:S(2)}) %all-to-all-start.1) | async-done | bytes 2097184 | tf_op jit(solution)/shard_map/all_to_all | solution.py:362
  178.9 5.4 %shard_map.119 = f32[128,4,4,256]{3,2,1,0:T(4,128)} custom-call(s32[32]{0:T(128)} %copy-done.22, f32[16,128,256]{2,1,0:T(8,128)} %copy-done.1, bf16[16,256,256]{2,1,0:T(8,128)(2,1)} %bitcast.35, bf16[64,128,128]{2,1,0:T(8,128)(2,1)} %bitcast.20.received), custom_call_target="tpu_custom_call" | custom-call | flops 268435456 | bytes 8388608 | tf_op jit(solution)/shard_map/pallas_call | solution.py:408
  (116 shorter events, 41.6 us)
Async XLA Ops:
  4.3 14.3 %copy-start.24 = (bf16[128,4,4,256]{3,2,1,0:T(4,128)(2,1)S(1)}, bf16[128,4,4,256]{3,2,1,0:T(4,128)(2,1)}, u32[]{:S(2)}) copy-start(bf16[128,4,4,256]{3,2,1,0:T(4,128)(2,1)} %param.10) | copy-start | bytes 3145732
  4.6 15.4 %copy-start.27 = (s32[1,4,4,2]{2,3,1,0:T(2,128)S(1)}, s32[1,4,4,2]{2,3,1,0:T(2,128)}, u32[]{:S(2)}) copy-start(s32[1,4,4,2]{2,3,1,0:T(2,128)} %param.14) | copy-start | bytes 388
  4.6 15.6 %copy-start.28 = (s32[64]{0:T(128)S(1)}, s32[64]{0:T(128)}, u32[]{:S(2)}) copy-start(s32[64]{0:T(128)} %param.16) | copy-start | bytes 772
  6.3 18.9 %collective-permute-start.2 = (f16[2,536,256]{2,1,0:T(8,128)(2,1)}, f16[2,536,256]{2,1,0:T(8,128)(2,1)}, u32[]{:S(2)}, u32[]{:S(2)}) collective-permute-start(f16[2,536,256]{2,1,0:T(8,128)(2,1)} %convert_element_type.55), channel_id=1, source_target_pairs={{0,32},{32,64},{64,96},{96,128},{128,160},{160,192},{192,224},{224... | collective-permute-start | bytes 1646600 | tf_op jit(solution)/shard_map/ppermute | solution.py:269
  8.8 15.4 %collective-permute-start.3 = (f16[2,536,256]{2,1,0:T(8,128)(2,1)}, f16[2,536,256]{2,1,0:T(8,128)(2,1)}, u32[]{:S(2)}, u32[]{:S(2)}) collective-permute-start(f16[2,536,256]{2,1,0:T(8,128)(2,1)} %convert_element_type.55), channel_id=1, source_target_pairs={{0,224},{32,0},{64,32},{96,64},{128,96},{160,128},{192,160},{224,1... | collective-permute-start | bytes 1646600 | tf_op jit(solution)/shard_map/ppermute | solution.py:269
  12.7 13.2 %collective-permute-start = (bf16[4,128,256]{2,1,0:T(8,128)(2,1)}, bf16[4,128,256]{2,1,0:T(8,128)(2,1)S(1)}, u32[]{:S(2)}, u32[]{:S(2)}) collective-permute-start(bf16[4,128,256]{2,1,0:T(8,128)(2,1)} %get-tuple-element.13), channel_id=1, source_target_pairs={{0,1},{1,2},{2,3},{3,4},{4,5},{5,6},{6,7},{7,8},{8,9},{9,10},{10,1... | collective-permute-start | bytes 786440 | tf_op jit(solution)/shard_map/ppermute | solution.py:269
  16.7 9.2 %collective-permute-start.1 = (bf16[4,128,256]{2,1,0:T(8,128)(2,1)}, bf16[4,128,256]{2,1,0:T(8,128)(2,1)}, u32[]{:S(2)}, u32[]{:S(2)}) collective-permute-start(bf16[4,128,256]{2,1,0:T(8,128)(2,1)} %get-tuple-element.14), channel_id=1, source_target_pairs={{1,0},{2,1},{3,2},{4,3},{5,4},{6,5},{7,6},{8,7},{9,8},{10,9},{11,1... | collective-permute-start | bytes 786440 | tf_op jit(solution)/shard_map/ppermute | solution.py:269
  20.6 11.1 %copy-start.22 = (s32[32]{0:T(128)}, s32[32]{0:T(128)S(1)}, u32[]{:S(2)}) copy-start(s32[32]{0:T(128)S(1)} %multiply_add_fusion.slot) | copy-start | bytes 388
  34.0 52.8 %all-to-all-start = ((bf16[32,264,128]{2,1,0:T(8,128)(2,1)}), bf16[32,264,128]{2,1,0:T(8,128)(2,1)S(1)}, u32[]{:S(2)}, u32[]{:S(2)}) async-start(bf16[32,264,128]{2,1,0:T(8,128)(2,1)} %copy-done.4), calls=%async_computation | async-start | bytes 4325376 | tf_op jit(solution)/shard_map/all_to_all | solution.py:362
  42.4 16.2 %collective-permute-start.6 = (f16[2,536,256]{2,1,0:T(8,128)(2,1)}, f16[2,536,256]{2,1,0:T(8,128)(2,1)S(1)}, u32[]{:S(2)}, u32[]{:S(2)}) collective-permute-start(f16[2,536,256]{2,1,0:T(8,128)(2,1)} %collective-permute-done.2), channel_id=1, source_target_pairs={{0,32},{32,64},{64,96},{96,128},{128,160},{160,192},{192,224},{224... | collective-permute-start | bytes 1646600 | tf_op jit(solution)/shard_map/ppermute | solution.py:269
  42.5 16.1 %collective-permute-start.4 = (f16[2,536,256]{2,1,0:T(8,128)(2,1)}, f16[2,536,256]{2,1,0:T(8,128)(2,1)S(1)}, u32[]{:S(2)}, u32[]{:S(2)}) collective-permute-start(f16[2,536,256]{2,1,0:T(8,128)(2,1)} %collective-permute-done.3), channel_id=1, source_target_pairs={{0,224},{32,0},{64,32},{96,64},{128,96},{160,128},{192,160},{224,1... | collective-permute-start | bytes 1646600 | tf_op jit(solution)/shard_map/ppermute | solution.py:269
  58.6 14.4 %collective-permute-start.7 = (f16[2,536,256]{2,1,0:T(8,128)(2,1)S(1)}, f16[2,536,256]{2,1,0:T(8,128)(2,1)S(1)}, u32[]{:S(2)}, u32[]{:S(2)}) collective-permute-start(f16[2,536,256]{2,1,0:T(8,128)(2,1)S(1)} %collective-permute-done.6), channel_id=1, source_target_pairs={{0,32},{32,64},{64,96},{96,128},{128,160},{160,192},{192,224},{224... | collective-permute-start | bytes 1646600 | tf_op jit(solution)/shard_map/ppermute | solution.py:269
  58.6 14.6 %collective-permute-start.5 = (f16[2,536,256]{2,1,0:T(8,128)(2,1)S(1)}, f16[2,536,256]{2,1,0:T(8,128)(2,1)S(1)}, u32[]{:S(2)}, u32[]{:S(2)}) collective-permute-start(f16[2,536,256]{2,1,0:T(8,128)(2,1)S(1)} %collective-permute-done.4), channel_id=1, source_target_pairs={{0,224},{32,0},{64,32},{96,64},{128,96},{160,128},{192,160},{224,1... | collective-permute-start | bytes 1646600 | tf_op jit(solution)/shard_map/ppermute | solution.py:269
  73.1 12.7 %collective-permute-start.8 = (f16[1,536,256]{2,1,0:T(8,128)(2,1)S(1)}, f16[1,536,256]{2,1,0:T(8,128)(2,1)S(1)}, u32[]{:S(2)}, u32[]{:S(2)}) collective-permute-start(f16[1,536,256]{2,1,0:T(8,128)(2,1)S(1)} %slice.42), channel_id=1, source_target_pairs={{0,32},{32,64},{64,96},{96,128},{128,160},{160,192},{192,224},{224... | collective-permute-start | bytes 823304 | tf_op jit(solution)/shard_map/ppermute | solution.py:269
  73.2 12.6 %collective-permute-start.9 = (f16[1,536,256]{2,1,0:T(8,128)(2,1)S(1)}, f16[1,536,256]{2,1,0:T(8,128)(2,1)S(1)}, u32[]{:S(2)}, u32[]{:S(2)}) collective-permute-start(f16[1,536,256]{2,1,0:T(8,128)(2,1)S(1)} %slice.43), channel_id=1, source_target_pairs={{0,224},{32,0},{64,32},{96,64},{128,96},{160,128},{192,160},{224,1... | collective-permute-start | bytes 823304 | tf_op jit(solution)/shard_map/ppermute | solution.py:269
  89.2 22.5 %collective-permute-start.10 = (bf16[2,128,256]{2,1,0:T(8,128)(2,1)}, bf16[2,128,256]{2,1,0:T(8,128)(2,1)S(1)}, u32[]{:S(2)}, u32[]{:S(2)}) collective-permute-start(bf16[2,128,256]{2,1,0:T(8,128)(2,1)} %get-tuple-element.21.refs_0_), channel_id=1, source_target_pairs={{0,224},{32,0},{64,32},{96,64},{128,96},{160,128},{192,160},{224,1... | collective-permute-start | bytes 393224 | tf_op jit(solution)/shard_map/ppermute | solution.py:269
  89.2 23.9 %collective-permute-start.11 = (bf16[2,128,256]{2,1,0:T(8,128)(2,1)}, bf16[2,128,256]{2,1,0:T(8,128)(2,1)S(1)}, u32[]{:S(2)}, u32[]{:S(2)}) collective-permute-start(bf16[2,128,256]{2,1,0:T(8,128)(2,1)} %get-tuple-element.21.refs_0_), channel_id=1, source_target_pairs={{0,192},{32,224},{64,0},{96,32},{128,64},{160,96},{192,128},{224,1... | collective-permute-start | bytes 393224 | tf_op jit(solution)/shard_map/ppermute | solution.py:269
  108.4 11.1 %collective-permute-start.12 = (bf16[2,128,256]{2,1,0:T(8,128)(2,1)}, bf16[2,128,256]{2,1,0:T(8,128)(2,1)S(1)}, u32[]{:S(2)}, u32[]{:S(2)}) collective-permute-start(bf16[2,128,256]{2,1,0:T(8,128)(2,1)} %get-tuple-element.21.refs_0_), channel_id=1, source_target_pairs={{0,160},{32,192},{64,224},{96,0},{128,32},{160,64},{192,96},{224,1... | collective-permute-start | bytes 393224 | tf_op jit(solution)/shard_map/ppermute | solution.py:269
  108.4 11.1 %collective-permute-start.13 = (bf16[2,128,256]{2,1,0:T(8,128)(2,1)}, bf16[2,128,256]{2,1,0:T(8,128)(2,1)S(1)}, u32[]{:S(2)}, u32[]{:S(2)}) collective-permute-start(bf16[2,128,256]{2,1,0:T(8,128)(2,1)} %get-tuple-element.21.refs_0_), channel_id=1, source_target_pairs={{0,128},{32,160},{64,192},{96,224},{128,0},{160,32},{192,64},{224,... | collective-permute-start | bytes 393224 | tf_op jit(solution)/shard_map/ppermute | solution.py:269
  111.4 17.7 %collective-permute-start.14 = (bf16[2,128,256]{2,1,0:T(8,128)(2,1)}, bf16[2,128,256]{2,1,0:T(8,128)(2,1)S(1)}, u32[]{:S(2)}, u32[]{:S(2)}) collective-permute-start(bf16[2,128,256]{2,1,0:T(8,128)(2,1)} %get-tuple-element.21.refs_0_), channel_id=1, source_target_pairs={{0,96},{32,128},{64,160},{96,192},{128,224},{160,0},{192,32},{224,... | collective-permute-start | bytes 393224 | tf_op jit(solution)/shard_map/ppermute | solution.py:269
  111.7 17.4 %collective-permute-start.15 = (bf16[2,128,256]{2,1,0:T(8,128)(2,1)}, bf16[2,128,256]{2,1,0:T(8,128)(2,1)S(1)}, u32[]{:S(2)}, u32[]{:S(2)}) collective-permute-start(bf16[2,128,256]{2,1,0:T(8,128)(2,1)} %get-tuple-element.21.refs_0_), channel_id=1, source_target_pairs={{0,64},{32,96},{64,128},{96,160},{128,192},{160,224},{192,0},{224,... | collective-permute-start | bytes 393224 | tf_op jit(solution)/shard_map/ppermute | solution.py:269
  113.7 22.2 %collective-permute-start.16 = (bf16[2,128,256]{2,1,0:T(8,128)(2,1)}, bf16[2,128,256]{2,1,0:T(8,128)(2,1)S(1)}, u32[]{:S(2)}, u32[]{:S(2)}) collective-permute-start(bf16[2,128,256]{2,1,0:T(8,128)(2,1)} %get-tuple-element.21.refs_0_), channel_id=1, source_target_pairs={{0,32},{32,64},{64,96},{96,128},{128,160},{160,192},{192,224},{224... | collective-permute-start | bytes 393224 | tf_op jit(solution)/shard_map/ppermute | solution.py:269
  142.3 7.8 %copy-start.17 = (bf16[16,128,256]{2,1,0:T(8,128)(2,1)S(1)}, bf16[16,128,256]{2,1,0:T(8,128)(2,1)}, u32[]{:S(2)}) copy-start(bf16[16,128,256]{2,1,0:T(8,128)(2,1)} %copy-done.16) | copy-start | bytes 3145732
  142.3 36.5 %all-to-all-start.1 = ((bf16[32,2,128,128]{3,2,1,0:T(8,128)(2,1)}), bf16[32,2,128,128]{3,2,1,0:T(8,128)(2,1)}, u32[]{:S(2)}, u32[]{:S(2)}) async-start(bf16[32,2,128,128]{3,2,1,0:T(8,128)(2,1)} %bitcast.40), calls=%async_computation.1 | async-start | bytes 4194304 | tf_op jit(solution)/shard_map/all_to_all | solution.py:362
  (24 other events, 57.3 us)

commit v3 on v2

--- a/solution.py
+++ b/solution.py
@@ -12,7 +12,8 @@
 F32 = jnp.float32
 BF16 = jnp.bfloat16
 MIB = 1 << 20
-FACTOR_MIB = 24
+FACTOR_MIB = 56
+SOLVE_MIB = 56
 
 
 def dot(a, b, kind):
@@ -34,7 +35,7 @@
     return dot(left, right, kind)
 
 
-def leaf_kernel(extent_y, slot, volt, source, diag, below, above, left, right, blocks, marks, low_out, sent):
+def leaf_kernel(extent_y, slot, volt, source, diag, below, above, edge, blocks, marks, low_out, sent):
     panels, fields, width = volt.shape
     rows = sent.shape[2]
     per_leaf = slot.shape[0] // panels
@@ -42,8 +43,8 @@
     sent[:, : capacity * fields, :] = jnp.zeros((sent.shape[0], capacity * fields, rows), BF16)
     sent[:, capacity * fields :, :] = marks[...]
     lane = lax.broadcasted_iota(jnp.int32, (fields, width), 1)
-    rest = jnp.zeros((fields - 2 * panels, left.shape[1]), F32)
-    sides = jnp.transpose(jnp.concatenate([left[...], right[...], rest], axis=0))
+    rest = jnp.zeros((fields - 2 * panels, edge.shape[1]), F32)
+    sides = jnp.transpose(jnp.concatenate([edge[...], rest], axis=0))
     for p in range(panels):
         y = p % extent_y
         center = volt[p].astype(F32)
@@ -178,18 +179,27 @@
     lax.fori_loop(0, columns - 1, up, last)
 
 
-def solve_kernel(columns, tag, m_high, m_low, *refs):
-    drives, (result, sent, low) = refs[:columns], refs[columns:]
-    sep_rows, fields, width = result.shape
+def solve_kernel(columns, tag, m_high_in, m_low_in, *refs):
+    drives, (result, sent, m_high, m_low, low, sems) = refs[:columns], refs[columns:]
+    sep_rows, _, width = result.shape
     rows = sent.shape[2]
     halves = width // rows
+    loads = []
+    for k in range(columns):
+        one = pltpu.make_async_copy(m_high_in.at[k], m_high.at[k], sems.at[2 * k])
+        two = pltpu.make_async_copy(m_low_in.at[k], m_low.at[k], sems.at[2 * k + 1])
+        one.start()
+        two.start()
+        loads.append((one, two))
+    for k in range(columns):
+        for load in loads[k]:
+            load.wait()
+        for e in range(sep_rows):
+            d = drives[k][e]
+            term = dot(d, m_high[k, e], "nt") + dot(d, m_low[k, e], "nt")
+            result[e] = term if k == 0 else result[e] + term
     for e in range(sep_rows):
-        acc = jnp.zeros((fields, width), F32)
-        for k in range(columns):
-            d = drives[k][e]
-            acc = acc + dot(d, m_high[k, e], "nt") + dot(d, m_low[k, e], "nt")
-        result[e] = acc
-        narrow = acc.astype(BF16)
+        narrow = result[e].astype(BF16)
         for h in range(halves):
             low[e * halves + h] = narrow[:, h * rows : (h + 1) * rows]
 
@@ -312,10 +322,11 @@
         pieces[columns - hop] = up
         pieces[hop] = down
     column = lax.axis_index("col")
-    left = pieces[columns - 1][0, 2 * width + 8 :, :fields].astype(F32)
-    left = jnp.where(column > 0, left, 0.0)
-    right = pieces[1][0, 2 * width + 8 :, fields : 2 * fields].astype(F32)
-    right = jnp.where(column < columns - 1, right, 0.0)
+    far = 2 * width + 8
+    ids = jnp.arange(2 * panels, dtype=jnp.int32)[:, None]
+    inside = jnp.where(ids < panels, column > 0, column < columns - 1)
+    edge = jnp.concatenate([pieces[columns - 1][0, far:, :fields], pieces[1][0, far:, fields : 2 * fields]], axis=0)
+    edge = jnp.where(inside, edge.astype(F32), 0.0)
     middle = sep_rows // 2
     up = shifted(up[:middle], "col", 1, True)
     down = shifted(down[middle:], "col", -1, True)
@@ -330,7 +341,7 @@
     low, sent = call(
         functools.partial(leaf_kernel, extent_y),
         (shape((panels, fields, width), BF16), shape((owners, capacity * fields + 8, rows), BF16)),
-        [SM] + [VM] * 9,
+        [SM] + [VM] * 8,
         (VM, VM),
         12,
         flops=2 * panels * fields * width * width,
@@ -342,8 +353,7 @@
         (6.0 + conduct).reshape(panels, width),
         below,
         above,
-        left,
-        right,
+        edge,
         blocks,
         marks,
     )
@@ -392,15 +402,27 @@
     )(place, *pieces)
 
     drives = [drive] * columns
-    for k in sorted(range(1, columns), key=lambda k: -min(k, columns - k)):
+    for k in (1, 2):
         drives[k] = shifted(drive, "col", -k, True)
+        drives[columns - k] = shifted(drive, "col", k, True)
+    ahead, behind = drives[2], drives[columns - 2]
+    drives[3] = shifted(ahead, "col", -1, True)
+    drives[columns - 3] = shifted(behind, "col", 1, True)
+    low_part = shifted(ahead[:middle], "col", -2, True)
+    high_part = shifted(behind[middle:], "col", 2, True)
+    drives[4] = jnp.concatenate([low_part, high_part], axis=0)
     result, answer = call(
         functools.partial(solve_kernel, columns),
         (shape((sep_rows, fields, width), F32), shape((slots, fields, rows), BF16)),
-        [SM] + [VM] * (2 + columns),
+        [SM] + [HB] * 2 + [VM] * columns,
         (VM, VM),
-        10,
-        scratch=[pltpu.VMEM((sep_rows * halves, fields, rows), BF16)],
+        SOLVE_MIB,
+        scratch=[
+            pltpu.VMEM(square.shape, BF16),
+            pltpu.VMEM(square.shape, BF16),
+            pltpu.VMEM((sep_rows * halves, fields, rows), BF16),
+            pltpu.SemaphoreType.DMA((2 * columns,)),
+        ],
         flops=4 * columns * sep_rows * fields * width * width,
         moved=8 << 20,
     )(in_tags, m_high, m_low, *drives)

time: 185 us -> 169 us (0.914)
  waiting for transfers between devices: 72.3 us -> 58.6 us
  local copies, waits for them, and re-layouts: 29 us -> 19.9 us
  Pallas kernels: 24.3 us -> 29.2 us
  starting transfers between devices: 45.1 us -> 47.7 us
    ppermute x17 -> x18, waiting for transfers between devices: 46.6 us -> 33 us  [shifted(): return lax.ppermute(block, axis, route)]
    unnamed x63 -> x53, local copies, waits for them, and re-layouts: 24 us -> 13 us
    pallas_call x1, Pallas kernels: 2.61 us -> 5.84 us  [level(): call(functools.partial(solve_kernel, columns), (shape((sep_rows, fields,...]
    pallas_call x1, Pallas kernels: 9.8 us -> 12.1 us  [level(): call(functools.partial(factor_kernel, columns), (square, square), [SM] +...]
    ppermute x17 -> x18, starting transfers between devices: 29 us -> 30 us  [shifted(): return lax.ppermute(block, axis, route)]
  transfers between devices with their start and end apart: 19 -> 20, of which waited for: 8 -> 6; matrix products, arithmetic and copies ran while one was open for 10% -> 13% of each run, Pallas kernels for 6% -> 9%
where the time goes in v3:
time: 169 us
  waiting for transfers between devices  58.6 us (35%)
  starting transfers between devices  47.7 us (28%)
  Pallas kernels  29.2 us (17%)
  local copies, waits for them, and re-layouts  19.9 us (12%)
  other arithmetic  12 us (7%)
    ppermute x18, waiting for transfers between devices, shifted(): return lax.ppermute(block, axis, route)  33 us
    ppermute x18, starting transfers between devices, shifted(): return lax.ppermute(block, axis, route)  30 us
    all_to_all x2, waiting for transfers between devices, exchange(): lax.all_to_all(block, 'leaf', split_axis=0, concat_axis=0, tiled=True)  25.6 us
    all_to_all x2, starting transfers between devices, exchange(): lax.all_to_all(block, 'leaf', split_axis=0, concat_axis=0, tiled=True)  17.7 us
    unnamed x53, local copies, waits for them, and re-layouts  13 us
    pallas_call x1, Pallas kernels, level(): call(functools.partial(factor_kernel, columns), (square, square), [SM] +...  12.1 us
    convert_element_type x6, other arithmetic, level(): pieces[k] = pieces[k].astype(F32)  8.71 us
    pallas_call x1, Pallas kernels, level(): call(functools.partial(solve_kernel, columns), (shape((sep_rows, fields,...  5.84 us
  transfers between devices with their start and end apart: 20, of which 6 were waited for; matrix products, arithmetic and copies ran while one was open for 13% of the time, Pallas kernels for 9%

profile of v3, /device:TPU:1, one launch (start us, length us, event | category | flops | bytes accessed | tf_op | source)
XLA Modules:
  0.0 168.7 jit_solution(15208017568241675630)
XLA Ops:
  5.8 2.5 %collective-permute-start.2 = (f16[2,536,256]{2,1,0:T(8,128)(2,1)}, f16[2,536,256]{2,1,0:T(8,128)(2,1)}, u32[]{:S(2)}, u32[]{:S(2)}) collective-permute-start(f16[2,536,256]{2,1,0:T(8,128)(2,1)} %convert_element_type.50), channel_id=1, source_target_pairs={{0,32},{32,64},{64,96},{96,128},{128,160},{160,192},{192,224},{224... | collective-permute-start | bytes 1646600 | tf_op jit(solution)/shard_map/ppermute | solution.py:279
  8.2 3.9 %collective-permute-start.3 = (f16[2,536,256]{2,1,0:T(8,128)(2,1)}, f16[2,536,256]{2,1,0:T(8,128)(2,1)}, u32[]{:S(2)}, u32[]{:S(2)}) collective-permute-start(f16[2,536,256]{2,1,0:T(8,128)(2,1)} %convert_element_type.50), channel_id=1, source_target_pairs={{0,224},{32,0},{64,32},{96,64},{128,96},{160,128},{192,160},{224,1... | collective-permute-start | bytes 1646600 | tf_op jit(solution)/shard_map/ppermute | solution.py:279
  12.2 3.9 %collective-permute-start = (bf16[4,128,256]{2,1,0:T(8,128)(2,1)}, bf16[4,128,256]{2,1,0:T(8,128)(2,1)S(1)}, u32[]{:S(2)}, u32[]{:S(2)}) collective-permute-start(bf16[4,128,256]{2,1,0:T(8,128)(2,1)} %get-tuple-element.13), channel_id=1, source_target_pairs={{0,1},{1,2},{2,3},{3,4},{4,5},{5,6},{6,7},{7,8},{8,9},{9,10},{10,1... | collective-permute-start | bytes 786440 | tf_op jit(solution)/shard_map/ppermute | solution.py:279
  18.8 2.7 %copy.31 = bf16[128,4,4,256]{3,0,2,1:T(8,128)(2,1)} copy(bf16[128,4,4,256]{3,2,1,0:T(4,128)(2,1)} %param.10) | data formatting | bytes 2097152 | tf_op args[0]
  21.6 2.6 %copy.32 = bf16[128,4,4,256]{3,0,2,1:T(8,128)(2,1)} copy(bf16[128,4,4,256]{3,2,1,0:T(4,128)(2,1)} %param.11) | data formatting | bytes 2097152 | tf_op args[1]
  27.1 3.3 %shard_map.114 = (bf16[16,128,256]{2,1,0:T(8,128)(2,1)S(1)}, bf16[32,264,128]{2,1,0:T(8,128)(2,1)S(1)}) custom-call(s32[32]{0:T(128)S(1)} %multiply_add_fusion.slot, bf16[16,128,256]{2,1,0:T(8,128)(2,1)S(1)} %bitcast.37, bf16[16,128,256]{2,1,0:T(8,128)(2,1)S(1)} %bitcast.38, f32[16,256]{1,0:T(8,128)S(1)} %reshape.166.diag, ...), custom_call_target="tpu_custom_call" | custom-call | flops 268435456 | bytes 8388608 | tf_op jit(solution)/shard_map/pallas_call | solution.py:341
  32.7 8.0 %all-to-all-start = ((bf16[32,264,128]{2,1,0:T(8,128)(2,1)}), bf16[32,264,128]{2,1,0:T(8,128)(2,1)S(1)}, u32[]{:S(2)}, u32[]{:S(2)}) async-start(bf16[32,264,128]{2,1,0:T(8,128)(2,1)} %copy-done.5), calls=%async_computation | async-start | bytes 4325376 | tf_op jit(solution)/shard_map/all_to_all | solution.py:372
  40.8 3.4 %collective-permute-start.4 = (f16[2,536,256]{2,1,0:T(8,128)(2,1)}, f16[2,536,256]{2,1,0:T(8,128)(2,1)S(1)}, u32[]{:S(2)}, u32[]{:S(2)}) collective-permute-start(f16[2,536,256]{2,1,0:T(8,128)(2,1)} %collective-permute-done.3), channel_id=1, source_target_pairs={{0,224},{32,0},{64,32},{96,64},{128,96},{160,128},{192,160},{224,1... | collective-permute-start | bytes 1646600 | tf_op jit(solution)/shard_map/ppermute | solution.py:279
  44.2 12.7 %collective-permute-done.6 = f16[2,536,256]{2,1,0:T(8,128)(2,1)S(1)} collective-permute-done((f16[2,536,256]{2,1,0:T(8,128)(2,1)}, f16[2,536,256]{2,1,0:T(8,128)(2,1)S(1)}, u32[]{:S(2)}, u32[]{:S(2)}) %collective-permute-start.6) | collective-permute-done | bytes 548896 | tf_op jit(solution)/shard_map/ppermute | solution.py:279
  57.0 2.7 %collective-permute-start.5 = (f16[2,536,256]{2,1,0:T(8,128)(2,1)S(1)}, f16[2,536,256]{2,1,0:T(8,128)(2,1)S(1)}, u32[]{:S(2)}, u32[]{:S(2)}) collective-permute-start(f16[2,536,256]{2,1,0:T(8,128)(2,1)S(1)} %collective-permute-done.4), channel_id=1, source_target_pairs={{0,224},{32,0},{64,32},{96,64},{128,96},{160,128},{192,160},{224,1... | collective-permute-start | bytes 1646600 | tf_op jit(solution)/shard_map/ppermute | solution.py:279
  59.6 11.7 %collective-permute-done.7 = f16[2,536,256]{2,1,0:T(8,128)(2,1)S(1)} collective-permute-done((f16[2,536,256]{2,1,0:T(8,128)(2,1)S(1)}, f16[2,536,256]{2,1,0:T(8,128)(2,1)S(1)}, u32[]{:S(2)}, u32[]{:S(2)}) %collective-permute-start.7) | collective-permute-done | bytes 548896 | tf_op jit(solution)/shard_map/ppermute | solution.py:279
  72.3 2.7 %collective-permute-start.9 = (f16[1,536,256]{2,1,0:T(8,128)(2,1)}, f16[1,536,256]{2,1,0:T(8,128)(2,1)S(1)}, u32[]{:S(2)}, u32[]{:S(2)}) collective-permute-start(f16[1,536,256]{2,1,0:T(8,128)(2,1)} %slice.51), channel_id=1, source_target_pairs={{0,224},{32,0},{64,32},{96,64},{128,96},{160,128},{192,160},{224,1... | collective-permute-start | bytes 823304 | tf_op jit(solution)/shard_map/ppermute | solution.py:279
  75.9 2.1 %convert_element_type.56.refs_1_ = f32[2,536,256]{2,1,0:T(8,128)} convert(f16[2,536,256]{2,1,0:T(8,128)(2,1)} %collective-permute-done.3) | non-fusion elementwise | flops 274432 | bytes 1646592 | tf_op jit(solution)/shard_map/convert_element_type | solution.py:335
  87.4 2.3 %collective-permute-start.14 = (bf16[2,128,256]{2,1,0:T(8,128)(2,1)S(1)}, bf16[2,128,256]{2,1,0:T(8,128)(2,1)S(1)}, u32[]{:S(2)}, u32[]{:S(2)}) collective-permute-start(bf16[2,128,256]{2,1,0:T(8,128)(2,1)S(1)} %get-tuple-element.21.refs_0_), channel_id=1, source_target_pairs={{0,64},{32,96},{64,128},{96,160},{128,192},{160,224},{192,0},{224,... | collective-permute-start | bytes 393224 | tf_op jit(solution)/shard_map/ppermute | solution.py:279
  89.8 2.3 %collective-permute-done.11.refs_2_ = bf16[2,128,256]{2,1,0:T(8,128)(2,1)S(1)} collective-permute-done((bf16[2,128,256]{2,1,0:T(8,128)(2,1)S(1)}, bf16[2,128,256]{2,1,0:T(8,128)(2,1)S(1)}, u32[]{:S(2)}, u32[]{:S(2)}) %collective-permute-start.11) | collective-permute-done | bytes 131104 | tf_op jit(solution)/shard_map/ppermute | solution.py:279
  92.1 2.4 %collective-permute-start.13 = (bf16[1,128,256]{2,1,0:T(8,128)(2,1)S(1)}, bf16[1,128,256]{2,1,0:T(8,128)(2,1)S(1)}, u32[]{:S(2)}, u32[]{:S(2)}) collective-permute-start(bf16[1,128,256]{2,1,0:T(8,128)(2,1)S(1)} %slice.52), channel_id=1, source_target_pairs={{0,192},{32,224},{64,0},{96,32},{128,64},{160,96},{192,128},{224,1... | collective-permute-start | bytes 196616 | tf_op jit(solution)/shard_map/ppermute | solution.py:279
  94.4 12.1 %shard_map.117 = (bf16[8,2,256,256]{3,2,1,0:T(8,128)(2,1)}, bf16[8,2,256,256]{3,2,1,0:T(8,128)(2,1)}) custom-call(s32[1]{0:T(128)} %bitcast.18.place, f32[2,536,256]{2,1,0:T(8,128)} %copy-done.2, f32[2,536,256]{2,1,0:T(8,128)} %convert_element_type.56.refs_1_, f32[2,536,256]{2,1,0:T(8,128)} %convert_element_type.57.refs_2_, ...), custom_call_target="tpu_custom_call" | custom-call | flops 4227858432 | bytes 12582912 | tf_op jit(solution)/shard_map/pallas_call | solution.py:388
  108.2 2.4 %collective-permute-start.12 = (bf16[2,128,256]{2,1,0:T(8,128)(2,1)S(1)}, bf16[2,128,256]{2,1,0:T(8,128)(2,1)S(1)}, u32[]{:S(2)}, u32[]{:S(2)}) collective-permute-start(bf16[2,128,256]{2,1,0:T(8,128)(2,1)S(1)} %collective-permute-done.11.refs_2_), channel_id=1, source_target_pairs={{0,224},{32,0},{64,32},{96,64},{128,96},{160,128},{192,160},{224,1... | collective-permute-start | bytes 393224 | tf_op jit(solution)/shard_map/ppermute | solution.py:279
  111.2 3.3 %collective-permute-done.15 = bf16[1,128,256]{2,1,0:T(8,128)(2,1)S(1)} collective-permute-done((bf16[1,128,256]{2,1,0:T(8,128)(2,1)S(1)}, bf16[1,128,256]{2,1,0:T(8,128)(2,1)S(1)}, u32[]{:S(2)}, u32[]{:S(2)}) %collective-permute-start.15) | collective-permute-done | bytes 65568 | tf_op jit(solution)/shard_map/ppermute | solution.py:279
  115.3 2.9 %collective-permute-done.16.refs_5_ = bf16[2,128,256]{2,1,0:T(8,128)(2,1)S(1)} collective-permute-done((bf16[2,128,256]{2,1,0:T(8,128)(2,1)S(1)}, bf16[2,128,256]{2,1,0:T(8,128)(2,1)S(1)}, u32[]{:S(2)}, u32[]{:S(2)}) %collective-permute-start.16) | collective-permute-done | bytes 131104 | tf_op jit(solution)/shard_map/ppermute | solution.py:279
  118.8 5.8 %shard_map.118 = (f32[2,128,256]{2,1,0:T(8,128)}, bf16[64,128,128]{2,1,0:T(8,128)(2,1)}) custom-call(s32[64]{0:T(128)} %convert_element_type.55.tag, bf16[8,2,256,256]{3,2,1,0:T(8,128)(2,1)} %get-tuple-element.19.m_high_in, bf16[8,2,256,256]{3,2,1,0:T(8,128)(2,1)} %get-tuple-element.20.m_low_in, bf16[2,128,256]{2,1,0:T(8,128)(2,1)} %copy-done.11, ...), custom_call_target="tpu_custom_call" | custom-call | flops 536870912 | bytes 8388608 | tf_op jit(solution)/shard_map/pallas_call | solution.py:414
  124.7 9.8 %all-to-all-start.1 = ((bf16[32,2,128,128]{3,2,1,0:T(8,128)(2,1)}), bf16[32,2,128,128]{3,2,1,0:T(8,128)(2,1)}, u32[]{:S(2)}, u32[]{:S(2)}) async-start(bf16[32,2,128,128]{3,2,1,0:T(8,128)(2,1)} %bitcast.43), calls=%async_computation.1 | async-start | bytes 4194304 | tf_op jit(solution)/shard_map/all_to_all | solution.py:372
  137.6 25.6 %all-to-all-done.1 = bf16[32,2,128,128]{3,2,1,0:T(8,128)(2,1)} async-done(((bf16[32,2,128,128]{3,2,1,0:T(8,128)(2,1)}), bf16[32,2,128,128]{3,2,1,0:T(8,128)(2,1)}, u32[]{:S(2)}, u32[]{:S(2)}) %all-to-all-start.1) | async-done | bytes 2097184 | tf_op jit(solution)/shard_map/all_to_all | solution.py:372
  163.2 5.4 %shard_map.119 = f32[128,4,4,256]{3,2,1,0:T(4,128)} custom-call(s32[32]{0:T(128)} %copy-done.12, f32[16,128,256]{2,1,0:T(8,128)} %copy-done.1, bf16[16,256,256]{2,1,0:T(8,128)(2,1)} %bitcast.35, bf16[64,128,128]{2,1,0:T(8,128)(2,1)} %bitcast.20.received), custom_call_target="tpu_custom_call" | custom-call | flops 268435456 | bytes 8388608 | tf_op jit(solution)/shard_map/pallas_call | solution.py:430
  (113 shorter events, 30.9 us)
Async XLA Ops:
  3.6 15.0 %copy-start.21 = (f32[4,4,256]{2,1,0:T(4,128)S(1)}, f32[4,4,256]{2,1,0:T(4,128)}, u32[]{:S(2)}) copy-start(f32[4,4,256]{2,1,0:T(4,128)} %param.12) | copy-start | bytes 49156
  3.9 17.6 %copy-start.2 = (f32[2,536,256]{2,1,0:T(8,128)}, f32[2,536,256]{2,1,0:T(8,128)S(1)}, u32[]{:S(2)}) copy-start(f32[2,536,256]{2,1,0:T(8,128)S(1)} %shard_map.113.refs_0_) | copy-start | bytes 3293188
  5.8 19.2 %collective-permute-start.2 = (f16[2,536,256]{2,1,0:T(8,128)(2,1)}, f16[2,536,256]{2,1,0:T(8,128)(2,1)}, u32[]{:S(2)}, u32[]{:S(2)}) collective-permute-start(f16[2,536,256]{2,1,0:T(8,128)(2,1)} %convert_element_type.50), channel_id=1, source_target_pairs={{0,32},{32,64},{64,96},{96,128},{128,160},{160,192},{192,224},{224... | collective-permute-start | bytes 1646600 | tf_op jit(solution)/shard_map/ppermute | solution.py:279
  8.2 16.1 %collective-permute-start.3 = (f16[2,536,256]{2,1,0:T(8,128)(2,1)}, f16[2,536,256]{2,1,0:T(8,128)(2,1)}, u32[]{:S(2)}, u32[]{:S(2)}) collective-permute-start(f16[2,536,256]{2,1,0:T(8,128)(2,1)} %convert_element_type.50), channel_id=1, source_target_pairs={{0,224},{32,0},{64,32},{96,64},{128,96},{160,128},{192,160},{224,1... | collective-permute-start | bytes 1646600 | tf_op jit(solution)/shard_map/ppermute | solution.py:279
  12.2 13.6 %collective-permute-start = (bf16[4,128,256]{2,1,0:T(8,128)(2,1)}, bf16[4,128,256]{2,1,0:T(8,128)(2,1)S(1)}, u32[]{:S(2)}, u32[]{:S(2)}) collective-permute-start(bf16[4,128,256]{2,1,0:T(8,128)(2,1)} %get-tuple-element.13), channel_id=1, source_target_pairs={{0,1},{1,2},{2,3},{3,4},{4,5},{5,6},{6,7},{7,8},{8,9},{9,10},{10,1... | collective-permute-start | bytes 786440 | tf_op jit(solution)/shard_map/ppermute | solution.py:279
  16.1 9.6 %collective-permute-start.1 = (bf16[4,128,256]{2,1,0:T(8,128)(2,1)}, bf16[4,128,256]{2,1,0:T(8,128)(2,1)}, u32[]{:S(2)}, u32[]{:S(2)}) collective-permute-start(bf16[4,128,256]{2,1,0:T(8,128)(2,1)} %get-tuple-element.14), channel_id=1, source_target_pairs={{1,0},{2,1},{3,2},{4,3},{5,4},{6,5},{7,6},{8,7},{9,8},{10,9},{11,1... | collective-permute-start | bytes 786440 | tf_op jit(solution)/shard_map/ppermute | solution.py:279
  32.7 51.9 %all-to-all-start = ((bf16[32,264,128]{2,1,0:T(8,128)(2,1)}), bf16[32,264,128]{2,1,0:T(8,128)(2,1)S(1)}, u32[]{:S(2)}, u32[]{:S(2)}) async-start(bf16[32,264,128]{2,1,0:T(8,128)(2,1)} %copy-done.5), calls=%async_computation | async-start | bytes 4325376 | tf_op jit(solution)/shard_map/all_to_all | solution.py:372
  40.7 16.2 %collective-permute-start.6 = (f16[2,536,256]{2,1,0:T(8,128)(2,1)}, f16[2,536,256]{2,1,0:T(8,128)(2,1)S(1)}, u32[]{:S(2)}, u32[]{:S(2)}) collective-permute-start(f16[2,536,256]{2,1,0:T(8,128)(2,1)} %collective-permute-done.2), channel_id=1, source_target_pairs={{0,32},{32,64},{64,96},{96,128},{128,160},{160,192},{192,224},{224... | collective-permute-start | bytes 1646600 | tf_op jit(solution)/shard_map/ppermute | solution.py:279
  40.8 16.1 %collective-permute-start.4 = (f16[2,536,256]{2,1,0:T(8,128)(2,1)}, f16[2,536,256]{2,1,0:T(8,128)(2,1)S(1)}, u32[]{:S(2)}, u32[]{:S(2)}) collective-permute-start(f16[2,536,256]{2,1,0:T(8,128)(2,1)} %collective-permute-done.3), channel_id=1, source_target_pairs={{0,224},{32,0},{64,32},{96,64},{128,96},{160,128},{192,160},{224,1... | collective-permute-start | bytes 1646600 | tf_op jit(solution)/shard_map/ppermute | solution.py:279
  57.0 14.4 %collective-permute-start.7 = (f16[2,536,256]{2,1,0:T(8,128)(2,1)S(1)}, f16[2,536,256]{2,1,0:T(8,128)(2,1)S(1)}, u32[]{:S(2)}, u32[]{:S(2)}) collective-permute-start(f16[2,536,256]{2,1,0:T(8,128)(2,1)S(1)} %collective-permute-done.6), channel_id=1, source_target_pairs={{0,32},{32,64},{64,96},{96,128},{128,160},{160,192},{192,224},{224... | collective-permute-start | bytes 1646600 | tf_op jit(solution)/shard_map/ppermute | solution.py:279
  57.0 14.6 %collective-permute-start.5 = (f16[2,536,256]{2,1,0:T(8,128)(2,1)S(1)}, f16[2,536,256]{2,1,0:T(8,128)(2,1)S(1)}, u32[]{:S(2)}, u32[]{:S(2)}) collective-permute-start(f16[2,536,256]{2,1,0:T(8,128)(2,1)S(1)} %collective-permute-done.4), channel_id=1, source_target_pairs={{0,224},{32,0},{64,32},{96,64},{128,96},{160,128},{192,160},{224,1... | collective-permute-start | bytes 1646600 | tf_op jit(solution)/shard_map/ppermute | solution.py:279
  71.4 14.9 %collective-permute-start.8 = (f16[1,536,256]{2,1,0:T(8,128)(2,1)S(1)}, f16[1,536,256]{2,1,0:T(8,128)(2,1)S(1)}, u32[]{:S(2)}, u32[]{:S(2)}) collective-permute-start(f16[1,536,256]{2,1,0:T(8,128)(2,1)S(1)} %slice.50), channel_id=1, source_target_pairs={{0,32},{32,64},{64,96},{96,128},{128,160},{160,192},{192,224},{224... | collective-permute-start | bytes 823304 | tf_op jit(solution)/shard_map/ppermute | solution.py:279
  72.3 14.1 %collective-permute-start.9 = (f16[1,536,256]{2,1,0:T(8,128)(2,1)}, f16[1,536,256]{2,1,0:T(8,128)(2,1)S(1)}, u32[]{:S(2)}, u32[]{:S(2)}) collective-permute-start(f16[1,536,256]{2,1,0:T(8,128)(2,1)} %slice.51), channel_id=1, source_target_pairs={{0,224},{32,0},{64,32},{96,64},{128,96},{160,128},{192,160},{224,1... | collective-permute-start | bytes 823304 | tf_op jit(solution)/shard_map/ppermute | solution.py:279
  86.2 20.4 %copy-start.11 = (bf16[2,128,256]{2,1,0:T(8,128)(2,1)}, bf16[2,128,256]{2,1,0:T(8,128)(2,1)S(1)}, u32[]{:S(2)}) copy-start(bf16[2,128,256]{2,1,0:T(8,128)(2,1)S(1)} %get-tuple-element.21.refs_0_) | copy-start | bytes 393220
  86.2 5.8 %collective-permute-start.11 = (bf16[2,128,256]{2,1,0:T(8,128)(2,1)S(1)}, bf16[2,128,256]{2,1,0:T(8,128)(2,1)S(1)}, u32[]{:S(2)}, u32[]{:S(2)}) collective-permute-start(bf16[2,128,256]{2,1,0:T(8,128)(2,1)S(1)} %get-tuple-element.21.refs_0_), channel_id=1, source_target_pairs={{0,192},{32,224},{64,0},{96,32},{128,64},{160,96},{192,128},{224,1... | collective-permute-start | bytes 393224 | tf_op jit(solution)/shard_map/ppermute | solution.py:279
  87.4 20.7 %collective-permute-start.14 = (bf16[2,128,256]{2,1,0:T(8,128)(2,1)S(1)}, bf16[2,128,256]{2,1,0:T(8,128)(2,1)S(1)}, u32[]{:S(2)}, u32[]{:S(2)}) collective-permute-start(bf16[2,128,256]{2,1,0:T(8,128)(2,1)S(1)} %get-tuple-element.21.refs_0_), channel_id=1, source_target_pairs={{0,64},{32,96},{64,128},{96,160},{128,192},{160,224},{192,0},{224,... | collective-permute-start | bytes 393224 | tf_op jit(solution)/shard_map/ppermute | solution.py:279
  92.1 16.1 %copy-start.14 = (bf16[2,128,256]{2,1,0:T(8,128)(2,1)}, bf16[2,128,256]{2,1,0:T(8,128)(2,1)S(1)}, u32[]{:S(2)}) copy-start(bf16[2,128,256]{2,1,0:T(8,128)(2,1)S(1)} %collective-permute-done.11.refs_2_) | copy-start | bytes 393220
  92.1 18.5 %collective-permute-start.13 = (bf16[1,128,256]{2,1,0:T(8,128)(2,1)S(1)}, bf16[1,128,256]{2,1,0:T(8,128)(2,1)S(1)}, u32[]{:S(2)}, u32[]{:S(2)}) collective-permute-start(bf16[1,128,256]{2,1,0:T(8,128)(2,1)S(1)} %slice.52), channel_id=1, source_target_pairs={{0,192},{32,224},{64,0},{96,32},{128,64},{160,96},{192,128},{224,1... | collective-permute-start | bytes 196616 | tf_op jit(solution)/shard_map/ppermute | solution.py:279
  106.5 8.7 %collective-permute-start.10 = (bf16[2,128,256]{2,1,0:T(8,128)(2,1)S(1)}, bf16[2,128,256]{2,1,0:T(8,128)(2,1)S(1)}, u32[]{:S(2)}, u32[]{:S(2)}) collective-permute-start(bf16[2,128,256]{2,1,0:T(8,128)(2,1)S(1)} %get-tuple-element.21.refs_0_), channel_id=1, source_target_pairs={{0,224},{32,0},{64,32},{96,64},{128,96},{160,128},{192,160},{224,1... | collective-permute-start | bytes 393224 | tf_op jit(solution)/shard_map/ppermute | solution.py:279
  106.6 8.6 %collective-permute-start.17 = (bf16[2,128,256]{2,1,0:T(8,128)(2,1)S(1)}, bf16[2,128,256]{2,1,0:T(8,128)(2,1)S(1)}, u32[]{:S(2)}, u32[]{:S(2)}) collective-permute-start(bf16[2,128,256]{2,1,0:T(8,128)(2,1)S(1)} %get-tuple-element.21.refs_0_), channel_id=1, source_target_pairs={{0,32},{32,64},{64,96},{96,128},{128,160},{160,192},{192,224},{224... | collective-permute-start | bytes 393224 | tf_op jit(solution)/shard_map/ppermute | solution.py:279
  108.1 6.5 %collective-permute-start.15 = (bf16[1,128,256]{2,1,0:T(8,128)(2,1)S(1)}, bf16[1,128,256]{2,1,0:T(8,128)(2,1)S(1)}, u32[]{:S(2)}, u32[]{:S(2)}) collective-permute-start(bf16[1,128,256]{2,1,0:T(8,128)(2,1)S(1)} %slice.53), channel_id=1, source_target_pairs={{0,64},{32,96},{64,128},{96,160},{128,192},{160,224},{192,0},{224,... | collective-permute-start | bytes 196616 | tf_op jit(solution)/shard_map/ppermute | solution.py:279
  108.2 7.1 %collective-permute-start.12 = (bf16[2,128,256]{2,1,0:T(8,128)(2,1)S(1)}, bf16[2,128,256]{2,1,0:T(8,128)(2,1)S(1)}, u32[]{:S(2)}, u32[]{:S(2)}) collective-permute-start(bf16[2,128,256]{2,1,0:T(8,128)(2,1)S(1)} %collective-permute-done.11.refs_2_), channel_id=1, source_target_pairs={{0,224},{32,0},{64,32},{96,64},{128,96},{160,128},{192,160},{224,1... | collective-permute-start | bytes 393224 | tf_op jit(solution)/shard_map/ppermute | solution.py:279
  110.6 7.6 %collective-permute-start.16 = (bf16[2,128,256]{2,1,0:T(8,128)(2,1)S(1)}, bf16[2,128,256]{2,1,0:T(8,128)(2,1)S(1)}, u32[]{:S(2)}, u32[]{:S(2)}) collective-permute-start(bf16[2,128,256]{2,1,0:T(8,128)(2,1)S(1)} %collective-permute-done.14.refs_6_), channel_id=1, source_target_pairs={{0,32},{32,64},{64,96},{96,128},{128,160},{160,192},{192,224},{224... | collective-permute-start | bytes 393224 | tf_op jit(solution)/shard_map/ppermute | solution.py:279
  124.7 38.5 %all-to-all-start.1 = ((bf16[32,2,128,128]{3,2,1,0:T(8,128)(2,1)}), bf16[32,2,128,128]{3,2,1,0:T(8,128)(2,1)}, u32[]{:S(2)}, u32[]{:S(2)}) async-start(bf16[32,2,128,128]{3,2,1,0:T(8,128)(2,1)} %bitcast.43), calls=%async_computation.1 | async-start | bytes 4194304 | tf_op jit(solution)/shard_map/all_to_all | solution.py:372
  (20 other events, 101.6 us)

commit v4 on v3

--- a/solution.py
+++ b/solution.py
@@ -123,7 +123,7 @@
 
 
 def factor_kernel(columns, place, *refs):
-    pieces, (m_high, m_low, ring, z, y, sems) = refs[:columns], refs[columns:]
+    pieces, (high_out, low_out, m_high, m_low, ring, z, y, sems, out_sems) = refs[:columns], refs[columns:]
     chains, _, width = pieces[0].shape
     copies = [pltpu.make_async_copy(pieces[k], ring.at[k], sems.at[k]) for k in range(columns)]
     for copy in copies:
@@ -162,6 +162,8 @@
             high, low = split(xs[e])
             m_high[rel, e] = high
             m_low[rel, e] = low
+        pltpu.make_async_copy(m_high.at[rel], high_out.at[rel], out_sems.at[rel]).start()
+        pltpu.make_async_copy(m_low.at[rel], low_out.at[rel], out_sems.at[columns + rel]).start()
 
     last = tuple(z[columns - 1, e] for e in range(chains))
     put(columns - 1, last)
@@ -177,10 +179,13 @@
         return tuple(out)
 
     lax.fori_loop(0, columns - 1, up, last)
+    for k in range(columns):
+        pltpu.make_async_copy(m_high.at[k], high_out.at[k], out_sems.at[k]).wait()
+        pltpu.make_async_copy(m_low.at[k], low_out.at[k], out_sems.at[columns + k]).wait()
 
 
 def solve_kernel(columns, tag, m_high_in, m_low_in, *refs):
-    drives, (result, sent, m_high, m_low, low, sems) = refs[:columns], refs[columns:]
+    drives, (extra, result, sent, m_high, m_low, low, sems) = refs[:columns], refs[columns:]
     sep_rows, _, width = result.shape
     rows = sent.shape[2]
     halves = width // rows
@@ -195,7 +200,8 @@
         for load in loads[k]:
             load.wait()
         for e in range(sep_rows):
-            d = drives[k][e]
+            half = drives[k].shape[0]
+            d = drives[k][e] if e < half else extra[e - half]
             term = dot(d, m_high[k, e], "nt") + dot(d, m_low[k, e], "nt")
             result[e] = term if k == 0 else result[e] + term
     for e in range(sep_rows):
@@ -389,13 +395,16 @@
         functools.partial(factor_kernel, columns),
         (square, square),
         [SM] + [HB] * columns,
-        (VM, VM),
+        (HB, HB),
         FACTOR_MIB,
         scratch=[
+            pltpu.VMEM(square.shape, BF16),
+            pltpu.VMEM(square.shape, BF16),
             pltpu.VMEM((columns,) + packed.shape, F32),
             pltpu.VMEM((columns, sep_rows, width, width), F32),
             pltpu.VMEM((sep_rows, width, width), F32),
             pltpu.SemaphoreType.DMA((columns,)),
+            pltpu.SemaphoreType.DMA((2 * columns,)),
         ],
         flops=2 * 126 * width**3,
         moved=12 << 20,
@@ -410,11 +419,11 @@
     drives[columns - 3] = shifted(behind, "col", 1, True)
     low_part = shifted(ahead[:middle], "col", -2, True)
     high_part = shifted(behind[middle:], "col", 2, True)
-    drives[4] = jnp.concatenate([low_part, high_part], axis=0)
+    drives[columns // 2] = low_part
     result, answer = call(
         functools.partial(solve_kernel, columns),
         (shape((sep_rows, fields, width), F32), shape((slots, fields, rows), BF16)),
-        [SM] + [HB] * 2 + [VM] * columns,
+        [SM] + [HB] * 2 + [VM] * (columns + 1),
         (VM, VM),
         SOLVE_MIB,
         scratch=[
@@ -425,7 +434,7 @@
         ],
         flops=4 * columns * sep_rows * fields * width * width,
         moved=8 << 20,
-    )(in_tags, m_high, m_low, *drives)
+    )(in_tags, m_high, m_low, *drives, high_part)
     returned = exchange(answer.reshape(owners, capacity, fields, rows)).reshape(slots, fields, rows)
     leaf_result = call(
         functools.partial(finish_kernel, extent_y),

time: 169 us -> 166 us (0.982)
  starting transfers between devices: 47.7 us -> 51.7 us
  waiting for transfers between devices: 58.6 us -> 54.7 us
  local copies, waits for them, and re-layouts: 19.9 us -> 18.2 us
    ppermute x18, waiting for transfers between devices: 33 us -> 29.1 us  [shifted(): return lax.ppermute(block, axis, route)]
    all_to_all x2, starting transfers between devices: 17.7 us -> 20.1 us  [exchange(): lax.all_to_all(block, 'leaf', split_axis=0, concat_axis=0, tiled=True)]
    unnamed x53 -> x59, local copies, waits for them, and re-layouts: 13 us -> 12 us
  transfers between devices with their start and end apart: 20 -> 20, of which waited for: 6 -> 5; matrix products, arithmetic and copies ran while one was open for 13% -> 12% of each run, Pallas kernels for 9% -> 7%
where the time goes in v4:
time: 166 us
  waiting for transfers between devices  54.7 us (33%)
  starting transfers between devices  51.7 us (31%)
  Pallas kernels  28.2 us (17%)
  local copies, waits for them, and re-layouts  18.2 us (11%)
  other arithmetic  11.4 us (7%)
    ppermute x18, starting transfers between devices, shifted(): return lax.ppermute(block, axis, route)  31.6 us
    ppermute x18, waiting for transfers between devices, shifted(): return lax.ppermute(block, axis, route)  29.1 us
    all_to_all x2, waiting for transfers between devices, exchange(): lax.all_to_all(block, 'leaf', split_axis=0, concat_axis=0, tiled=True)  25.6 us
    all_to_all x2, starting transfers between devices, exchange(): lax.all_to_all(block, 'leaf', split_axis=0, concat_axis=0, tiled=True)  20.1 us
    unnamed x59, local copies, waits for them, and re-layouts  12 us
    pallas_call x1, Pallas kernels, level(): call(functools.partial(factor_kernel, columns), (square, square), [SM] +...  11.1 us
    convert_element_type x6, other arithmetic, level(): pieces[k] = pieces[k].astype(F32)  8.63 us
    pallas_call x1, Pallas kernels, level(): call(functools.partial(solve_kernel, columns), (shape((sep_rows, fields,...  5.82 us
  transfers between devices with their start and end apart: 20, of which 5 were waited for; matrix products, arithmetic and copies ran while one was open for 12% of the time, Pallas kernels for 7%

profile of v4, /device:TPU:1, one launch (start us, length us, event | category | flops | bytes accessed | tf_op | source)
XLA Modules:
  0.0 165.6 jit_solution(8762134239738210994)
XLA Ops:
  5.8 2.5 %collective-permute-start.2 = (f16[2,536,256]{2,1,0:T(8,128)(2,1)}, f16[2,536,256]{2,1,0:T(8,128)(2,1)}, u32[]{:S(2)}, u32[]{:S(2)}) collective-permute-start(f16[2,536,256]{2,1,0:T(8,128)(2,1)} %convert_element_type.50), channel_id=1, source_target_pairs={{0,32},{32,64},{64,96},{96,128},{128,160},{160,192},{192,224},{224... | collective-permute-start | bytes 1646600 | tf_op jit(solution)/shard_map/ppermute | solution.py:285
  8.2 3.9 %collective-permute-start.3 = (f16[2,536,256]{2,1,0:T(8,128)(2,1)}, f16[2,536,256]{2,1,0:T(8,128)(2,1)}, u32[]{:S(2)}, u32[]{:S(2)}) collective-permute-start(f16[2,536,256]{2,1,0:T(8,128)(2,1)} %convert_element_type.50), channel_id=1, source_target_pairs={{0,224},{32,0},{64,32},{96,64},{128,96},{160,128},{192,160},{224,1... | collective-permute-start | bytes 1646600 | tf_op jit(solution)/shard_map/ppermute | solution.py:285
  12.2 3.9 %collective-permute-start = (bf16[4,128,256]{2,1,0:T(8,128)(2,1)}, bf16[4,128,256]{2,1,0:T(8,128)(2,1)S(1)}, u32[]{:S(2)}, u32[]{:S(2)}) collective-permute-start(bf16[4,128,256]{2,1,0:T(8,128)(2,1)} %get-tuple-element.13), channel_id=1, source_target_pairs={{0,1},{1,2},{2,3},{3,4},{4,5},{5,6},{6,7},{7,8},{8,9},{9,10},{10,1... | collective-permute-start | bytes 786440 | tf_op jit(solution)/shard_map/ppermute | solution.py:285
  18.8 2.7 %copy.31 = bf16[128,4,4,256]{3,0,2,1:T(8,128)(2,1)} copy(bf16[128,4,4,256]{3,2,1,0:T(4,128)(2,1)} %param.10) | data formatting | bytes 2097152 | tf_op args[0]
  21.6 2.6 %copy.32 = bf16[128,4,4,256]{3,0,2,1:T(8,128)(2,1)} copy(bf16[128,4,4,256]{3,2,1,0:T(4,128)(2,1)} %param.11) | data formatting | bytes 2097152 | tf_op args[1]
  27.1 3.3 %shard_map.114 = (bf16[16,128,256]{2,1,0:T(8,128)(2,1)S(1)}, bf16[32,264,128]{2,1,0:T(8,128)(2,1)S(1)}) custom-call(s32[32]{0:T(128)S(1)} %multiply_add_fusion.slot, bf16[16,128,256]{2,1,0:T(8,128)(2,1)S(1)} %bitcast.37, bf16[16,128,256]{2,1,0:T(8,128)(2,1)S(1)} %bitcast.38, f32[16,256]{1,0:T(8,128)S(1)} %reshape.166.diag, ...), custom_call_target="tpu_custom_call" | custom-call | flops 268435456 | bytes 8388608 | tf_op jit(solution)/shard_map/pallas_call | solution.py:347
  32.8 8.1 %all-to-all-start = ((bf16[32,264,128]{2,1,0:T(8,128)(2,1)}), bf16[32,264,128]{2,1,0:T(8,128)(2,1)S(1)}, u32[]{:S(2)}, u32[]{:S(2)}) async-start(bf16[32,264,128]{2,1,0:T(8,128)(2,1)} %copy-done.5), calls=%async_computation | async-start | bytes 4325376 | tf_op jit(solution)/shard_map/all_to_all | solution.py:378
  41.0 3.4 %collective-permute-start.4 = (f16[2,536,256]{2,1,0:T(8,128)(2,1)}, f16[2,536,256]{2,1,0:T(8,128)(2,1)S(1)}, u32[]{:S(2)}, u32[]{:S(2)}) collective-permute-start(f16[2,536,256]{2,1,0:T(8,128)(2,1)} %collective-permute-done.3), channel_id=1, source_target_pairs={{0,224},{32,0},{64,32},{96,64},{128,96},{160,128},{192,160},{224,1... | collective-permute-start | bytes 1646600 | tf_op jit(solution)/shard_map/ppermute | solution.py:285
  44.4 12.7 %collective-permute-done.6 = f16[2,536,256]{2,1,0:T(8,128)(2,1)S(1)} collective-permute-done((f16[2,536,256]{2,1,0:T(8,128)(2,1)}, f16[2,536,256]{2,1,0:T(8,128)(2,1)S(1)}, u32[]{:S(2)}, u32[]{:S(2)}) %collective-permute-start.6) | collective-permute-done | bytes 548896 | tf_op jit(solution)/shard_map/ppermute | solution.py:285
  57.1 2.7 %collective-permute-start.5 = (f16[2,536,256]{2,1,0:T(8,128)(2,1)S(1)}, f16[2,536,256]{2,1,0:T(8,128)(2,1)S(1)}, u32[]{:S(2)}, u32[]{:S(2)}) collective-permute-start(f16[2,536,256]{2,1,0:T(8,128)(2,1)S(1)} %collective-permute-done.4), channel_id=1, source_target_pairs={{0,224},{32,0},{64,32},{96,64},{128,96},{160,128},{192,160},{224,1... | collective-permute-start | bytes 1646600 | tf_op jit(solution)/shard_map/ppermute | solution.py:285
  59.8 11.7 %collective-permute-done.7 = f16[2,536,256]{2,1,0:T(8,128)(2,1)S(1)} collective-permute-done((f16[2,536,256]{2,1,0:T(8,128)(2,1)S(1)}, f16[2,536,256]{2,1,0:T(8,128)(2,1)S(1)}, u32[]{:S(2)}, u32[]{:S(2)}) %collective-permute-start.7) | collective-permute-done | bytes 548896 | tf_op jit(solution)/shard_map/ppermute | solution.py:285
  71.7 2.9 %collective-permute-start.9 = (f16[1,536,256]{2,1,0:T(8,128)(2,1)S(1)}, f16[1,536,256]{2,1,0:T(8,128)(2,1)S(1)}, u32[]{:S(2)}, u32[]{:S(2)}) collective-permute-start(f16[1,536,256]{2,1,0:T(8,128)(2,1)S(1)} %slice.51), channel_id=1, source_target_pairs={{0,224},{32,0},{64,32},{96,64},{128,96},{160,128},{192,160},{224,1... | collective-permute-start | bytes 823304 | tf_op jit(solution)/shard_map/ppermute | solution.py:285
  74.7 2.1 %convert_element_type.56.refs_1_ = f32[2,536,256]{2,1,0:T(8,128)} convert(f16[2,536,256]{2,1,0:T(8,128)(2,1)} %collective-permute-done.3) | non-fusion elementwise | flops 274432 | bytes 1646592 | tf_op jit(solution)/shard_map/convert_element_type | solution.py:341
  76.8 2.2 %convert_element_type.61.refs_7_ = f32[2,536,256]{2,1,0:T(8,128)} convert(f16[2,536,256]{2,1,0:T(8,128)(2,1)} %collective-permute-done.2) | non-fusion elementwise | flops 274432 | bytes 1646592 | tf_op jit(solution)/shard_map/convert_element_type | solution.py:341
  86.2 2.4 %collective-permute-start.14 = (bf16[2,128,256]{2,1,0:T(8,128)(2,1)S(1)}, bf16[2,128,256]{2,1,0:T(8,128)(2,1)S(1)}, u32[]{:S(2)}, u32[]{:S(2)}) collective-permute-start(bf16[2,128,256]{2,1,0:T(8,128)(2,1)S(1)} %get-tuple-element.21.refs_0_), channel_id=1, source_target_pairs={{0,64},{32,96},{64,128},{96,160},{128,192},{160,224},{192,0},{224,... | collective-permute-start | bytes 393224 | tf_op jit(solution)/shard_map/ppermute | solution.py:285
  89.8 11.1 %shard_map.117 = (bf16[8,2,256,256]{3,2,1,0:T(8,128)(2,1)}, bf16[8,2,256,256]{3,2,1,0:T(8,128)(2,1)}) custom-call(s32[1]{0:T(128)} %bitcast.18.place, f32[2,536,256]{2,1,0:T(8,128)} %copy-done.2, f32[2,536,256]{2,1,0:T(8,128)} %convert_element_type.56.refs_1_, f32[2,536,256]{2,1,0:T(8,128)} %convert_element_type.57.refs_2_, ...), custom_call_target="tpu_custom_call" | custom-call | flops 4227858432 | bytes 12582912 | tf_op jit(solution)/shard_map/pallas_call | solution.py:394
  101.1 2.4 %collective-permute-start.17 = (bf16[1,128,256]{2,1,0:T(8,128)(2,1)S(1)}, bf16[1,128,256]{2,1,0:T(8,128)(2,1)S(1)}, u32[]{:S(2)}, u32[]{:S(2)}) collective-permute-start(bf16[1,128,256]{2,1,0:T(8,128)(2,1)S(1)} %slice.53), channel_id=1, source_target_pairs={{0,64},{32,96},{64,128},{96,160},{128,192},{160,224},{192,0},{224,... | collective-permute-start | bytes 196616 | tf_op jit(solution)/shard_map/ppermute | solution.py:285
  103.5 3.9 %collective-permute-start.12 = (bf16[2,128,256]{2,1,0:T(8,128)(2,1)S(1)}, bf16[2,128,256]{2,1,0:T(8,128)(2,1)S(1)}, u32[]{:S(2)}, u32[]{:S(2)}) collective-permute-start(bf16[2,128,256]{2,1,0:T(8,128)(2,1)S(1)} %collective-permute-done.11.refs_2_), channel_id=1, source_target_pairs={{0,224},{32,0},{64,32},{96,64},{128,96},{160,128},{192,160},{224,1... | collective-permute-start | bytes 393224 | tf_op jit(solution)/shard_map/ppermute | solution.py:285
  108.1 1.9 %collective-permute-done.12.refs_3_ = bf16[2,128,256]{2,1,0:T(8,128)(2,1)S(1)} collective-permute-done((bf16[2,128,256]{2,1,0:T(8,128)(2,1)S(1)}, bf16[2,128,256]{2,1,0:T(8,128)(2,1)S(1)}, u32[]{:S(2)}, u32[]{:S(2)}) %collective-permute-start.12) | collective-permute-done | bytes 131104 | tf_op jit(solution)/shard_map/ppermute | solution.py:285
  110.0 2.7 %collective-permute-done.15.refs_5_ = bf16[2,128,256]{2,1,0:T(8,128)(2,1)S(1)} collective-permute-done((bf16[2,128,256]{2,1,0:T(8,128)(2,1)S(1)}, bf16[2,128,256]{2,1,0:T(8,128)(2,1)S(1)}, u32[]{:S(2)}, u32[]{:S(2)}) %collective-permute-start.15) | collective-permute-done | bytes 131104 | tf_op jit(solution)/shard_map/ppermute | solution.py:285
  113.4 5.8 %shard_map.118 = (f32[2,128,256]{2,1,0:T(8,128)}, bf16[64,128,128]{2,1,0:T(8,128)(2,1)}) custom-call(s32[64]{0:T(128)} %convert_element_type.55.tag, bf16[8,2,256,256]{3,2,1,0:T(8,128)(2,1)} %get-tuple-element.19.m_high_in, bf16[8,2,256,256]{3,2,1,0:T(8,128)(2,1)} %get-tuple-element.20.m_low_in, bf16[2,128,256]{2,1,0:T(8,128)(2,1)} %copy-done.11, ...), custom_call_target="tpu_custom_call" | custom-call | flops 536870912 | bytes 8388608 | tf_op jit(solution)/shard_map/pallas_call | solution.py:423
  119.2 12.0 %all-to-all-start.1 = ((bf16[32,2,128,128]{3,2,1,0:T(8,128)(2,1)}), bf16[32,2,128,128]{3,2,1,0:T(8,128)(2,1)}, u32[]{:S(2)}, u32[]{:S(2)}) async-start(bf16[32,2,128,128]{3,2,1,0:T(8,128)(2,1)} %bitcast.43), calls=%async_computation.1 | async-start | bytes 4194304 | tf_op jit(solution)/shard_map/all_to_all | solution.py:378
  134.4 25.6 %all-to-all-done.1 = bf16[32,2,128,128]{3,2,1,0:T(8,128)(2,1)} async-done(((bf16[32,2,128,128]{3,2,1,0:T(8,128)(2,1)}), bf16[32,2,128,128]{3,2,1,0:T(8,128)(2,1)}, u32[]{:S(2)}, u32[]{:S(2)}) %all-to-all-start.1) | async-done | bytes 2097184 | tf_op jit(solution)/shard_map/all_to_all | solution.py:378
  160.0 5.4 %shard_map.119 = f32[128,4,4,256]{3,2,1,0:T(4,128)} custom-call(s32[32]{0:T(128)} %copy-done.12, f32[16,128,256]{2,1,0:T(8,128)} %copy-done.1, bf16[16,256,256]{2,1,0:T(8,128)(2,1)} %bitcast.35, bf16[64,128,128]{2,1,0:T(8,128)(2,1)} %bitcast.20.received), custom_call_target="tpu_custom_call" | custom-call | flops 268435456 | bytes 8388608 | tf_op jit(solution)/shard_map/pallas_call | solution.py:439
  (118 shorter events, 26.3 us)
Async XLA Ops:
  3.6 15.0 %copy-start.24 = (f32[4,4,256]{2,1,0:T(4,128)S(1)}, f32[4,4,256]{2,1,0:T(4,128)}, u32[]{:S(2)}) copy-start(f32[4,4,256]{2,1,0:T(4,128)} %param.12) | copy-start | bytes 49156
  3.9 17.6 %copy-start.2 = (f32[2,536,256]{2,1,0:T(8,128)}, f32[2,536,256]{2,1,0:T(8,128)S(1)}, u32[]{:S(2)}) copy-start(f32[2,536,256]{2,1,0:T(8,128)S(1)} %shard_map.113.refs_0_) | copy-start | bytes 3293188
  5.8 19.2 %collective-permute-start.2 = (f16[2,536,256]{2,1,0:T(8,128)(2,1)}, f16[2,536,256]{2,1,0:T(8,128)(2,1)}, u32[]{:S(2)}, u32[]{:S(2)}) collective-permute-start(f16[2,536,256]{2,1,0:T(8,128)(2,1)} %convert_element_type.50), channel_id=1, source_target_pairs={{0,32},{32,64},{64,96},{96,128},{128,160},{160,192},{192,224},{224... | collective-permute-start | bytes 1646600 | tf_op jit(solution)/shard_map/ppermute | solution.py:285
  8.2 16.1 %collective-permute-start.3 = (f16[2,536,256]{2,1,0:T(8,128)(2,1)}, f16[2,536,256]{2,1,0:T(8,128)(2,1)}, u32[]{:S(2)}, u32[]{:S(2)}) collective-permute-start(f16[2,536,256]{2,1,0:T(8,128)(2,1)} %convert_element_type.50), channel_id=1, source_target_pairs={{0,224},{32,0},{64,32},{96,64},{128,96},{160,128},{192,160},{224,1... | collective-permute-start | bytes 1646600 | tf_op jit(solution)/shard_map/ppermute | solution.py:285
  12.2 13.6 %collective-permute-start = (bf16[4,128,256]{2,1,0:T(8,128)(2,1)}, bf16[4,128,256]{2,1,0:T(8,128)(2,1)S(1)}, u32[]{:S(2)}, u32[]{:S(2)}) collective-permute-start(bf16[4,128,256]{2,1,0:T(8,128)(2,1)} %get-tuple-element.13), channel_id=1, source_target_pairs={{0,1},{1,2},{2,3},{3,4},{4,5},{5,6},{6,7},{7,8},{8,9},{9,10},{10,1... | collective-permute-start | bytes 786440 | tf_op jit(solution)/shard_map/ppermute | solution.py:285
  16.1 9.7 %collective-permute-start.1 = (bf16[4,128,256]{2,1,0:T(8,128)(2,1)}, bf16[4,128,256]{2,1,0:T(8,128)(2,1)}, u32[]{:S(2)}, u32[]{:S(2)}) collective-permute-start(bf16[4,128,256]{2,1,0:T(8,128)(2,1)} %get-tuple-element.14), channel_id=1, source_target_pairs={{1,0},{2,1},{3,2},{4,3},{5,4},{6,5},{7,6},{8,7},{9,8},{10,9},{11,1... | collective-permute-start | bytes 786440 | tf_op jit(solution)/shard_map/ppermute | solution.py:285
  32.8 41.9 %copy-start.16 = (f32[128,2,256]{2,1,0:T(2,128)S(1)}, f32[128,2,256]{2,1,0:T(2,128)}, u32[]{:S(2)}) copy-start(f32[128,2,256]{2,1,0:T(2,128)} %param.17) | copy-start | bytes 786436
  32.8 51.7 %all-to-all-start = ((bf16[32,264,128]{2,1,0:T(8,128)(2,1)}), bf16[32,264,128]{2,1,0:T(8,128)(2,1)S(1)}, u32[]{:S(2)}, u32[]{:S(2)}) async-start(bf16[32,264,128]{2,1,0:T(8,128)(2,1)} %copy-done.5), calls=%async_computation | async-start | bytes 4325376 | tf_op jit(solution)/shard_map/all_to_all | solution.py:378
  40.9 16.2 %collective-permute-start.6 = (f16[2,536,256]{2,1,0:T(8,128)(2,1)}, f16[2,536,256]{2,1,0:T(8,128)(2,1)S(1)}, u32[]{:S(2)}, u32[]{:S(2)}) collective-permute-start(f16[2,536,256]{2,1,0:T(8,128)(2,1)} %collective-permute-done.2), channel_id=1, source_target_pairs={{0,32},{32,64},{64,96},{96,128},{128,160},{160,192},{192,224},{224... | collective-permute-start | bytes 1646600 | tf_op jit(solution)/shard_map/ppermute | solution.py:285
  41.0 16.1 %collective-permute-start.4 = (f16[2,536,256]{2,1,0:T(8,128)(2,1)}, f16[2,536,256]{2,1,0:T(8,128)(2,1)S(1)}, u32[]{:S(2)}, u32[]{:S(2)}) collective-permute-start(f16[2,536,256]{2,1,0:T(8,128)(2,1)} %collective-permute-done.3), channel_id=1, source_target_pairs={{0,224},{32,0},{64,32},{96,64},{128,96},{160,128},{192,160},{224,1... | collective-permute-start | bytes 1646600 | tf_op jit(solution)/shard_map/ppermute | solution.py:285
  57.1 14.4 %collective-permute-start.7 = (f16[2,536,256]{2,1,0:T(8,128)(2,1)S(1)}, f16[2,536,256]{2,1,0:T(8,128)(2,1)S(1)}, u32[]{:S(2)}, u32[]{:S(2)}) collective-permute-start(f16[2,536,256]{2,1,0:T(8,128)(2,1)S(1)} %collective-permute-done.6), channel_id=1, source_target_pairs={{0,32},{32,64},{64,96},{96,128},{128,160},{160,192},{192,224},{224... | collective-permute-start | bytes 1646600 | tf_op jit(solution)/shard_map/ppermute | solution.py:285
  57.1 14.6 %collective-permute-start.5 = (f16[2,536,256]{2,1,0:T(8,128)(2,1)S(1)}, f16[2,536,256]{2,1,0:T(8,128)(2,1)S(1)}, u32[]{:S(2)}, u32[]{:S(2)}) collective-permute-start(f16[2,536,256]{2,1,0:T(8,128)(2,1)S(1)} %collective-permute-done.4), channel_id=1, source_target_pairs={{0,224},{32,0},{64,32},{96,64},{128,96},{160,128},{192,160},{224,1... | collective-permute-start | bytes 1646600 | tf_op jit(solution)/shard_map/ppermute | solution.py:285
  71.6 11.7 %collective-permute-start.8 = (f16[1,536,256]{2,1,0:T(8,128)(2,1)S(1)}, f16[1,536,256]{2,1,0:T(8,128)(2,1)S(1)}, u32[]{:S(2)}, u32[]{:S(2)}) collective-permute-start(f16[1,536,256]{2,1,0:T(8,128)(2,1)S(1)} %slice.50), channel_id=1, source_target_pairs={{0,32},{32,64},{64,96},{96,128},{128,160},{160,192},{192,224},{224... | collective-permute-start | bytes 823304 | tf_op jit(solution)/shard_map/ppermute | solution.py:285
  71.7 11.6 %collective-permute-start.9 = (f16[1,536,256]{2,1,0:T(8,128)(2,1)S(1)}, f16[1,536,256]{2,1,0:T(8,128)(2,1)S(1)}, u32[]{:S(2)}, u32[]{:S(2)}) collective-permute-start(f16[1,536,256]{2,1,0:T(8,128)(2,1)S(1)} %slice.51), channel_id=1, source_target_pairs={{0,224},{32,0},{64,32},{96,64},{128,96},{160,128},{192,160},{224,1... | collective-permute-start | bytes 823304 | tf_op jit(solution)/shard_map/ppermute | solution.py:285
  86.1 14.8 %copy-start.11 = (bf16[2,128,256]{2,1,0:T(8,128)(2,1)}, bf16[2,128,256]{2,1,0:T(8,128)(2,1)S(1)}, u32[]{:S(2)}) copy-start(bf16[2,128,256]{2,1,0:T(8,128)(2,1)S(1)} %get-tuple-element.21.refs_0_) | copy-start | bytes 393220
  86.1 14.9 %collective-permute-start.11 = (bf16[2,128,256]{2,1,0:T(8,128)(2,1)S(1)}, bf16[2,128,256]{2,1,0:T(8,128)(2,1)S(1)}, u32[]{:S(2)}, u32[]{:S(2)}) collective-permute-start(bf16[2,128,256]{2,1,0:T(8,128)(2,1)S(1)} %get-tuple-element.21.refs_0_), channel_id=1, source_target_pairs={{0,192},{32,224},{64,0},{96,32},{128,64},{160,96},{192,128},{224,1... | collective-permute-start | bytes 393224 | tf_op jit(solution)/shard_map/ppermute | solution.py:285
  86.2 14.9 %collective-permute-start.14 = (bf16[2,128,256]{2,1,0:T(8,128)(2,1)S(1)}, bf16[2,128,256]{2,1,0:T(8,128)(2,1)S(1)}, u32[]{:S(2)}, u32[]{:S(2)}) collective-permute-start(bf16[2,128,256]{2,1,0:T(8,128)(2,1)S(1)} %get-tuple-element.21.refs_0_), channel_id=1, source_target_pairs={{0,64},{32,96},{64,128},{96,160},{128,192},{160,224},{192,0},{224,... | collective-permute-start | bytes 393224 | tf_op jit(solution)/shard_map/ppermute | solution.py:285
  88.5 18.9 %collective-permute-start.10 = (bf16[2,128,256]{2,1,0:T(8,128)(2,1)S(1)}, bf16[2,128,256]{2,1,0:T(8,128)(2,1)S(1)}, u32[]{:S(2)}, u32[]{:S(2)}) collective-permute-start(bf16[2,128,256]{2,1,0:T(8,128)(2,1)S(1)} %get-tuple-element.21.refs_0_), channel_id=1, source_target_pairs={{0,224},{32,0},{64,32},{96,64},{128,96},{160,128},{192,160},{224,1... | collective-permute-start | bytes 393224 | tf_op jit(solution)/shard_map/ppermute | solution.py:285
  100.9 7.2 %collective-permute-start.16 = (bf16[2,128,256]{2,1,0:T(8,128)(2,1)S(1)}, bf16[2,128,256]{2,1,0:T(8,128)(2,1)S(1)}, u32[]{:S(2)}, u32[]{:S(2)}) collective-permute-start(bf16[2,128,256]{2,1,0:T(8,128)(2,1)S(1)} %get-tuple-element.21.refs_0_), channel_id=1, source_target_pairs={{0,32},{32,64},{64,96},{96,128},{128,160},{160,192},{192,224},{224... | collective-permute-start | bytes 393224 | tf_op jit(solution)/shard_map/ppermute | solution.py:285
  101.0 7.0 %collective-permute-start.13 = (bf16[1,128,256]{2,1,0:T(8,128)(2,1)S(1)}, bf16[1,128,256]{2,1,0:T(8,128)(2,1)S(1)}, u32[]{:S(2)}, u32[]{:S(2)}) collective-permute-start(bf16[1,128,256]{2,1,0:T(8,128)(2,1)S(1)} %slice.52), channel_id=1, source_target_pairs={{0,192},{32,224},{64,0},{96,32},{128,64},{160,96},{192,128},{224,1... | collective-permute-start | bytes 196616 | tf_op jit(solution)/shard_map/ppermute | solution.py:285
  101.1 6.9 %collective-permute-start.17 = (bf16[1,128,256]{2,1,0:T(8,128)(2,1)S(1)}, bf16[1,128,256]{2,1,0:T(8,128)(2,1)S(1)}, u32[]{:S(2)}, u32[]{:S(2)}) collective-permute-start(bf16[1,128,256]{2,1,0:T(8,128)(2,1)S(1)} %slice.53), channel_id=1, source_target_pairs={{0,64},{32,96},{64,128},{96,160},{128,192},{160,224},{192,0},{224,... | collective-permute-start | bytes 196616 | tf_op jit(solution)/shard_map/ppermute | solution.py:285
  103.5 6.5 %collective-permute-start.12 = (bf16[2,128,256]{2,1,0:T(8,128)(2,1)S(1)}, bf16[2,128,256]{2,1,0:T(8,128)(2,1)S(1)}, u32[]{:S(2)}, u32[]{:S(2)}) collective-permute-start(bf16[2,128,256]{2,1,0:T(8,128)(2,1)S(1)} %collective-permute-done.11.refs_2_), channel_id=1, source_target_pairs={{0,224},{32,0},{64,32},{96,64},{128,96},{160,128},{192,160},{224,1... | collective-permute-start | bytes 393224 | tf_op jit(solution)/shard_map/ppermute | solution.py:285
  107.4 5.3 %collective-permute-start.15 = (bf16[2,128,256]{2,1,0:T(8,128)(2,1)S(1)}, bf16[2,128,256]{2,1,0:T(8,128)(2,1)S(1)}, u32[]{:S(2)}, u32[]{:S(2)}) collective-permute-start(bf16[2,128,256]{2,1,0:T(8,128)(2,1)S(1)} %collective-permute-done.14.refs_6_), channel_id=1, source_target_pairs={{0,32},{32,64},{64,96},{96,128},{128,160},{160,192},{192,224},{224... | collective-permute-start | bytes 393224 | tf_op jit(solution)/shard_map/ppermute | solution.py:285
  119.2 40.8 %all-to-all-start.1 = ((bf16[32,2,128,128]{3,2,1,0:T(8,128)(2,1)}), bf16[32,2,128,128]{3,2,1,0:T(8,128)(2,1)}, u32[]{:S(2)}, u32[]{:S(2)}) async-start(bf16[32,2,128,128]{3,2,1,0:T(8,128)(2,1)} %bitcast.43), calls=%async_computation.1 | async-start | bytes 4194304 | tf_op jit(solution)/shard_map/all_to_all | solution.py:378
  (23 other events, 132.9 us)
